TPU v7x, 32 devices: a whole 2x2x4 slice. The times are simulated.
32 devices in a mesh: dp: 4 (over y, x), seq: 4 (over z), tensor: 2 (over core).
Axes of the slice: x: 2, y: 2, z: 4, core: 2. Of those that a mesh axis runs over, the one named last changes fastest.
Arguments:
- byte_ids: int32 [4, 4096], P('dp', 'seq'), may hold values from 0 to 255
- pad_lengths: int32 [4], P('dp'), may hold values from 0 to 2048
- table: bfloat16 [256, 2048], P(None, 'tensor'), may hold values from -6 to 6
- conv_weight: float32 [3, 2048], P(None, 'tensor'), may hold values from -4 to 4
- score_weight: float32 [2048], P('tensor'), may hold values from -0.25 to 0.25
- norm_gain: float32 [2048], P('tensor'), may hold values from 0.5 to 1.5
- query_weight: bfloat16 [2048, 1024], P('tensor'), may hold values from -0.125 to 0.125
- query_grad: bfloat16 [4, 2048, 1024], P('dp', 'seq'), may hold values from -6 to 6
Outputs:
- grad_table: bfloat16 [256, 2048], P(None, 'tensor')
- grad_conv: float32 [3, 2048], P(None, 'tensor')
- grad_score: float32 [2048], P('tensor')
- grad_gain: float32 [2048], P('tensor')
- grad_wq: bfloat16 [2048, 1024], P('tensor', 'seq')
All inputs are finite; a program needn't handle non-finite values.
Results may differ from a plain program's by a relative error of at most 0.0095.
Values may be sent and summed in bfloat16 or wider, within the bound.
A program may use at most 128 MiB of HBM per device.

v0:
```python
import functools

import jax
import jax.numpy as jnp
from jax import lax
from jax.experimental import pallas as pl
from jax.experimental.pallas import tpu as pltpu
from jax.sharding import PartitionSpec as P

D = 2048
EPS = 1e-06
F32 = jnp.float32
BF16 = jnp.bfloat16
OFFS = range(-2, 4)
CHUNK = 256

NN = (((1,), (0,)), ((), ()))
NT = (((1,), (1,)), ((), ()))
TN = (((0,), (0,)), ((), ()))


def mm(lhs, rhs, dims):
    return lax.dot_general(lhs, rhs, dims, preferred_element_type=F32)


def block_weights(start, total, rows):
    i = lax.broadcasted_iota(jnp.int32, (1, rows), 1)
    even = (i % 2) == 0
    inside = {o: (start + 2 * i + o >= 0) & (start + 2 * i + o < total) for o in OFFS}
    table = []
    for b in range(4):
        for p in range(2):
            row = {}
            for o in OFFS:
                if b == 0:
                    if o == p:
                        row[o] = jnp.where(inside[o], 1.0, 0.0)
                elif b == 1:
                    if o in (0, 1):
                        row[o] = jnp.where(inside[o], 0.5, 0.0)
                elif b == 3:
                    if o in (0, 1):
                        row[o] = jnp.where(inside[o], 0.25, 0.0)
                    else:
                        row[o] = jnp.where(inside[o] & (even if o > 1 else ~even), 0.25, 0.0)
                else:
                    d = o - p
                    if -2 <= d <= 2:
                        r = (start + 2 * i + p) % 3
                        row[o] = jnp.where(inside[o] & (r >= -d) & (r <= 2 - d), 1.0 / 3.0, 0.0)
            table.append(row)
    return table


def spread(idm, rows_of, tap):
    rows = idm.shape[1]
    v = lax.broadcasted_iota(jnp.int32, (256, rows), 0)
    acc = None
    for o in OFFS:
        at = o + tap + 2
        term = jnp.where(idm[at : at + 1, :] == v, rows_of[o], 0.0)
        acc = term if acc is None else acc + term
    return acc


def forward_kernel(
    pos_ref, idm_ref, p_ref, table_ref, cw_ref, gain_ref, wq_ref, g_ref,
    pooled_ref, ng_ref, wt_ref, sums_ref, rows_ref, grads_ref,
    wh, wl, r1, r2, sq, rd,
):
    start, limit, total = pos_ref[0], pos_ref[1], pos_ref[2]
    rows = idm_ref.shape[1]
    chans = table_ref.shape[1]
    idm = idm_ref[...]
    v = lax.broadcasted_iota(jnp.int32, (256, rows), 0)
    p = p_ref[...]
    hi = p.astype(BF16)
    rest = p - hi.astype(F32)
    mid = rest.astype(BF16)
    low = (rest - mid.astype(F32)).astype(BF16)
    p3 = jnp.concatenate([hi.astype(F32), mid.astype(F32), low.astype(F32)], axis=0).astype(BF16)
    picks = []
    for j in range(8):
        hot = jnp.where(idm[j : j + 1, :] == v, 1.0, 0.0).astype(BF16)
        g = mm(p3, hot, NN)
        picks.append(g[0:8] + g[8:16] + g[16:24])
    s = {o: picks[o + 2][0:1] + picks[o + 3][1:2] + picks[o + 4][2:3] for o in OFFS}
    weights = block_weights(start, total, rows)
    expo = []
    for row in weights:
        score = None
        for o in row:
            score = row[o] * s[o] if score is None else score + row[o] * s[o]
        expo.append(jnp.exp(score))
    probs = []
    for n in range(8):
        whole = expo[n % 2] + expo[2 + n % 2] + expo[4 + n % 2] + expo[6 + n % 2]
        probs.append(expo[n] / whole)
    a = {}
    for o in OFFS:
        acc = None
        for n in range(8):
            if o in weights[n]:
                term = probs[n] * weights[n][o]
                acc = term if acc is None else acc + term
        a[o] = 0.5 * acc
    rows_ref[...] = jnp.concatenate(probs, axis=0)
    for k in range(3):
        w = spread(idm, a, k)
        wt_ref[k] = w.astype(BF16)
        wf = w.T
        top = wf.astype(BF16)
        wh[k] = top
        wl[k] = (wf - top.astype(F32)).astype(BF16)
    keep = (start + 2 * lax.broadcasted_iota(jnp.int32, g_ref.shape, 0)) < limit
    grads_ref[...] = jnp.where(keep, g_ref[...].astype(F32), 0.0).astype(BF16)
    r1[...] = jnp.zeros_like(r1)
    r2[...] = jnp.zeros_like(r2)
    sq[...] = jnp.zeros_like(sq)
    rd[...] = jnp.zeros_like(rd)

    def step(c, carry):
        at = pl.ds(pl.multiple_of(c * CHUNK, CHUNK), CHUNK)
        tab = table_ref[:, at]
        cw = cw_ref[:, at]
        ng = mm(grads_ref[...], wq_ref[at, :], NT)
        pooled = None
        for k in range(3):
            part = cw[k : k + 1] * (mm(wh[k], tab, NN) + mm(wl[k], tab, NN))
            pooled = part if pooled is None else pooled + part
        pooled_ref[:, at] = pooled
        ng_ref[:, at] = ng
        gained = ng * gain_ref[:, at]
        square = pooled * pooled
        inner = pooled * gained
        sq[...] += square[:, 0:128] + square[:, 128:256]
        rd[...] += inner[:, 0:128] + inner[:, 128:256]
        gb = gained.astype(BF16)
        pb = pooled.astype(BF16)
        for k in range(3):
            tk = (tab.astype(F32) * cw[k : k + 1]).astype(BF16)
            r1[k] += mm(tk, gb, NT)
            r2[k] += mm(tk, pb, NT)
        return carry

    lax.fori_loop(0, chans // CHUNK, step, 0)
    out = []
    for r in (r1, r2):
        for o in OFFS:
            acc = None
            for k in range(3):
                at = o + k + 2
                term = jnp.where(idm[at : at + 1, :] == v, r[k], 0.0)
                acc = term if acc is None else acc + term
            out.append(jnp.sum(acc, axis=0, keepdims=True))
    out.append(jnp.sum(sq[...].T, axis=0, keepdims=True))
    out.append(jnp.sum(rd[...].T, axis=0, keepdims=True))
    out.append(jnp.zeros((2, rows), F32))
    sums_ref[...] = jnp.concatenate(out, axis=0)


def backward_kernel(
    pos_ref, idm_ref, sums_ref, rows_ref, table_ref, cw_ref, sw_ref, gain_ref,
    pooled_ref, ng_ref, wt_ref, grads_ref,
    query_ref, tab_ref, small_ref,
):
    start, total = pos_ref[0], pos_ref[2]
    rows = idm_ref.shape[1]
    chans = table_ref.shape[1]
    idm = idm_ref[...]
    sums = sums_ref[...]
    probs = rows_ref[...]
    square, inner = sums[12:13], sums[13:14]
    scale = lax.rsqrt(square / D + EPS)
    pull = scale * scale * scale * (inner / D)
    q = {o: scale * sums[o + 2 : o + 3] - pull * sums[o + 8 : o + 9] for o in OFFS}
    weights = block_weights(start, total, rows)
    pgrad = []
    for row in weights:
        acc = None
        for o in row:
            acc = row[o] * q[o] if acc is None else acc + row[o] * q[o]
        pgrad.append(0.5 * acc)
    sgrad = []
    for n in range(8):
        mean = None
        for m in range(n % 2, 8, 2):
            term = probs[m : m + 1] * pgrad[m]
            mean = term if mean is None else mean + term
        sgrad.append(probs[n : n + 1] * (pgrad[n] - mean))
    ds = {}
    for o in OFFS:
        acc = None
        for n in range(8):
            if o in weights[n]:
                term = sgrad[n] * weights[n][o]
                acc = term if acc is None else acc + term
        ds[o] = acc
    hist = [jnp.sum(spread(idm, ds, k), axis=1, keepdims=True) for k in range(3)]
    cols = jnp.concatenate([scale, pull, jnp.zeros((6, rows), F32)], axis=0).T
    scale_c, pull_c = cols[:, 0:1], cols[:, 1:2]

    for c in range(chans // CHUNK):
        at = pl.ds(c * CHUNK, CHUNK)
        tab = table_ref[:, at].astype(F32)
        cw = cw_ref[:, at]
        sw = sw_ref[:, at]
        gain = gain_ref[:, at]
        ps = pooled_ref[:, at] * scale_c
        ng = ng_ref[:, at]
        gain_term = jnp.sum(ng * ps, axis=0, keepdims=True)
        normed = (ps * gain).astype(BF16)
        query_ref[at, :] = mm(normed, grads_ref[...], TN).astype(query_ref.dtype)
        pg = (ng * gain * scale_c - pull_c * pooled_ref[:, at]).astype(BF16)
        total_t = None
        outs = []
        score = None
        for k in range(3):
            full = mm(wt_ref[k], pg, NN) + hist[k] * sw
            term = cw[k : k + 1] * full
            total_t = term if total_t is None else total_t + term
            outs.append(jnp.sum(full * tab, axis=0, keepdims=True))
            term = cw[k : k + 1] * jnp.sum(hist[k] * tab, axis=0, keepdims=True)
            score = term if score is None else score + term
        tab_ref[:, at] = total_t.astype(tab_ref.dtype)
        small_ref[:, at] = jnp.concatenate(
            outs + [score, gain_term, jnp.zeros((3, CHUNK), F32)], axis=0
        )


def body(
    byte_ids, pad_lengths, table, conv_weight, score_weight, norm_gain, query_weight, query_grad
):
    ids = byte_ids[0]
    count = ids.shape[0]
    rows = count // 2
    vocab, chans = table.shape
    width = query_grad.shape[2]
    n_seq = lax.axis_size("seq")
    total = count * n_seq
    start = lax.axis_index("seq") * count
    limit = total - pad_lengths[0]
    ends = n_seq - 1
    up = [(i, i + 1) for i in range(ends)]
    down = [(i + 1, i) for i in range(ends)]
    ids_ext = jnp.concatenate(
        [lax.ppermute(ids[count - 3 :], "seq", up), ids, lax.ppermute(ids[:3], "seq", down)]
    )
    pos_e = start + jnp.arange(-3, count + 3, dtype=jnp.int32)
    ids_ext = jnp.where((pos_e >= 0) & (pos_e < limit), ids_ext, -1)
    halves = ids_ext.reshape(rows + 3, 2).T
    idm = jnp.stack([halves[j % 2, j // 2 : j // 2 + rows] for j in range(8)])
    pos = jnp.stack([start, limit, jnp.full_like(start, total)]).astype(jnp.int32)

    part = jnp.dot(
        conv_weight * score_weight, table.astype(F32).T, precision=lax.Precision.HIGHEST
    )
    p = jnp.pad(lax.psum(part, "tensor"), ((0, 5), (0, 0)))

    vm = pl.BlockSpec(memory_space=pltpu.VMEM)
    sm = pl.BlockSpec(memory_space=pltpu.SMEM)
    sw = score_weight[None, :]
    gain = norm_gain[None, :]
    pooled, ng, wt, sums, probs, grads = pl.pallas_call(
        forward_kernel,
        out_shape=(
            jax.ShapeDtypeStruct((rows, chans), F32),
            jax.ShapeDtypeStruct((rows, chans), F32),
            jax.ShapeDtypeStruct((3, vocab, rows), BF16),
            jax.ShapeDtypeStruct((16, rows), F32),
            jax.ShapeDtypeStruct((8, rows), F32),
            jax.ShapeDtypeStruct((rows, width), BF16),
        ),
        in_specs=[sm] + [vm] * 7,
        out_specs=(vm,) * 6,
        scratch_shapes=[
            pltpu.VMEM((3, rows, vocab), BF16),
            pltpu.VMEM((3, rows, vocab), BF16),
            pltpu.VMEM((3, vocab, rows), F32),
            pltpu.VMEM((3, vocab, rows), F32),
            pltpu.VMEM((rows, 128), F32),
            pltpu.VMEM((rows, 128), F32),
        ],
        name="forward",
    )(pos, idm, p, table, conv_weight, gain, query_weight, query_grad[0])
    sums = lax.psum(sums, "tensor")
    query, tab, small = pl.pallas_call(
        backward_kernel,
        out_shape=(
            jax.ShapeDtypeStruct((chans, width), BF16),
            jax.ShapeDtypeStruct((vocab, chans), BF16),
            jax.ShapeDtypeStruct((8, chans), F32),
        ),
        in_specs=[sm] + [vm] * 11,
        out_specs=(vm,) * 3,
        name="backward",
    )(pos, idm, sums, probs, table, conv_weight, sw, gain, pooled, ng, wt, grads)

    share = lax.psum_scatter(query, "seq", scatter_dimension=1, tiled=True)
    query_out = lax.psum(share, "dp")
    tab_out = lax.psum(tab, ("dp", "seq"))
    small_out = lax.psum(small, ("dp", "seq"))
    return (tab_out, small_out[0:3], small_out[3], small_out[4], query_out)


def solution(mesh):
    return jax.shard_map(
        body,
        mesh=mesh,
        in_specs=(
            P("dp", "seq"),
            P("dp"),
            P(None, "tensor"),
            P(None, "tensor"),
            P("tensor"),
            P("tensor"),
            P("tensor", None),
            P("dp", "seq", None),
        ),
        out_specs=(
            P(None, "tensor"),
            P(None, "tensor"),
            P("tensor"),
            P("tensor"),
            P("tensor", "seq"),
        ),
        check_vma=False,
    )
```

profile of v0, /device:TPU:0, one launch (start us, length us, event | category | flops | bytes accessed | tf_op | source)
XLA Modules:
  0.0 247.5 jit_solution(8620221706620420042)
XLA Ops:
  8.0 0.0 reduce-scatter.2.cloned.1.call-start
  8.0 0.7 slice_bitcast_fusion
  8.8 1.3 collective-permute-start.1
  10.1 5.6 %collective-permute-start = (s32[3]{0:T(128)S(1)}, s32[3]{0:T(128)S(1)}, u32[]{:S(2)}, u32[]{:S(2)}) collective-permute-start(s32[3]{0:T(128)S(1)} %get-tuple-element.30), channel_id=1, source_target_pairs={{0,2},{2,4},{4,6},{1,3},{3,5},{5,7},{8,10},{10,12},{12,14},{9,11},... | collective-permute-start | bytes 44 | tf_op jit(solution)/shard_map/ppermute | solution.py:247
  16.3 1.6 fusion
  17.9 2.5 psum.35
  20.4 0.6 pad_add_fusion.1.pos_ref
  21.0 0.6 pad.4.p_ref
  21.6 0.0 collective-permute-done.1
  21.6 0.0 collective-permute-done
  21.6 0.8 concatenate.5
  22.3 0.2 concatenate.6
  22.5 0.1 copy.13
  22.7 0.1 fusion.5
  22.8 0.6 pad_add_fusion.idm_ref
  23.4 13.9 %forward.1 = (f32[512,1024]{1,0:T(8,128)}, f32[512,1024]{1,0:T(8,128)}, bf16[3,256,512]{2,1,0:T(8,128)(2,1)}, f32[16,512]{1,0:T(8,128)}, f32[8,512]{1,0:T(8,128)}, /*index=5*/bf16[512,1024]{1,0:T(8,128)(2,1)}) custom-call(s32[3]{0:T(128)} %pad_add_fusion.1.pos_ref, s32[8,512]{1,0:T(8,128)} %pad_add_fusion.idm_ref, f32[8,256]{1,0:T(8,128)} %pad.4.p_ref, ...), custom_call_target="tpu_custom_call" | custom-call | tf_op jit(solution)/shard_map/forward/pallas_call | solution.py:264
  37.3 4.7 %psum.36.sums_ref = f32[16,512]{1,0:T(8,128)} all-reduce(f32[16,512]{1,0:T(8,128)} %get-tuple-element.14), channel_id=1, replica_groups=mesh['dp'=4,'seq'=4,'tensor'=2] {'tensor'}, use_global_device_ids=true, to_apply=%region_1.2 | all-reduce | flops 8192 | bytes 65536 | tf_op jit(solution)/shard_map/psum | solution.py:286
  42.0 8.3 %backward.1 = (bf16[1024,1024]{1,0:T(8,128)(2,1)}, bf16[256,1024]{1,0:T(8,128)(2,1)}, f32[8,1024]{1,0:T(8,128)}) custom-call(s32[3]{0:T(128)} %pad_add_fusion.1.pos_ref, s32[8,512]{1,0:T(8,128)} %pad_add_fusion.idm_ref, f32[16,512]{1,0:T(8,128)} %psum.36.sums_ref, f32[8,512]{1,0:T(8,128)} %get-tuple-element.15.rows_ref, bf16[256,1024]{1,0:T(8,128)(2,1)} %table_ref.3, ...), custom_call_target="tpu_custom_call" | custom-call | tf_op jit(solution)/shard_map/backward/pallas_call | solution.py:287
  50.3 0.0 copy-start
  50.4 0.0 reduce-scatter.2.cloned.1.call-update
  50.4 0.0 all-reduce.4.cloned.1.call-start
  50.4 0.5 all-reduce.4.cloned.1.call-update
  51.0 0.0 all-reduce.6.cloned.1.call-start
  51.0 46.6 %reduce-scatter.2.cloned.1.call-done = bf16[1024,256]{1,0:T(8,128)(2,1)} async-done(((bf16[1024,1024]{1,0:T(8,128)(2,1)}), bf16[1024,256]{1,0:T(8,128)(2,1)}) %reduce-scatter.2.cloned.1.call-update) | async-done | bytes 524304 | tf_op jit(solution)/shard_map/reduce_scatter | solution.py:299
  97.6 0.0 all-reduce.6.cloned.1.call-update
  97.7 0.0 copy-done
  97.7 76.1 %psum.38 = f32[8,1024]{1,0:T(8,128)S(1)} all-reduce(f32[8,1024]{1,0:T(8,128)S(1)} %copy-done), channel_id=1, replica_groups=mesh['dp'=4,'seq'=4,'tensor'=2] {'dp','seq'}, use_global_device_ids=true, to_apply=%region_3.4 | all-reduce | flops 8192 | bytes 65536 | tf_op jit(solution)/shard_map/psum | solution.py:302
  173.8 0.6 slice.56
  174.4 0.6 fusion.4
  175.0 14.7 %all-reduce.4.cloned.1.call-done = bf16[256,1024]{1,0:T(8,128)(2,1)} async-done(((bf16[256,1024]{1,0:T(8,128)(2,1)}), bf16[256,1024]{1,0:T(8,128)(2,1)}) %all-reduce.4.cloned.1.call-update) | async-done | bytes 524304 | tf_op jit(solution)/shard_map/psum | solution.py:301
  189.7 46.6 %all-reduce.6.cloned.1.call-done = bf16[1024,256]{1,0:T(8,128)(2,1)} async-done(((bf16[1024,256]{1,0:T(8,128)(2,1)}), bf16[1024,256]{1,0:T(8,128)(2,1)}) %all-reduce.6.cloned.1.call-update) | async-done | bytes 524304 | tf_op jit(solution)/shard_map/psum | solution.py:300
  236.3 1.9 copy.17
  238.2 1.9 copy.18
  (1 shorter events, 0.0 us)
Async XLA Ops:
  8.0 89.6 %reduce-scatter.2.cloned.1.call-start = ((), (), s32[]{:S(2)}) async-start(), calls=%async_computation.2 | async-start | bytes 2621440 | tf_op jit(solution)/shard_map/reduce_scatter | solution.py:299
  8.8 12.8 %collective-permute-start.1 = (s32[3]{0:T(128)S(1)}, s32[3]{0:T(128)S(1)}, u32[]{:S(2)}, u32[]{:S(2)}) collective-permute-start(s32[3]{0:T(128)S(1)} %get-tuple-element.29), channel_id=1, source_target_pairs={{2,0},{4,2},{6,4},{3,1},{5,3},{7,5},{10,8},{12,10},{14,12},{11,9},... | collective-permute-start | bytes 44 | tf_op jit(solution)/shard_map/ppermute | solution.py:247
  10.1 11.5 %collective-permute-start = (s32[3]{0:T(128)S(1)}, s32[3]{0:T(128)S(1)}, u32[]{:S(2)}, u32[]{:S(2)}) collective-permute-start(s32[3]{0:T(128)S(1)} %get-tuple-element.30), channel_id=1, source_target_pairs={{0,2},{2,4},{4,6},{1,3},{3,5},{5,7},{8,10},{10,12},{12,14},{9,11},... | collective-permute-start | bytes 44 | tf_op jit(solution)/shard_map/ppermute | solution.py:247
  50.3 47.3 %copy-start = (f32[8,1024]{1,0:T(8,128)S(1)}, f32[8,1024]{1,0:T(8,128)}, u32[]{:S(2)}) copy-start(f32[8,1024]{1,0:T(8,128)} %get-tuple-element.21) | copy-start | bytes 98308
  50.4 139.3 %all-reduce.4.cloned.1.call-start = ((), (), s32[]{:S(2)}) async-start(), calls=%async_computation.1 | async-start | bytes 1048576 | tf_op jit(solution)/shard_map/psum | solution.py:301
  51.0 185.3 %all-reduce.6.cloned.1.call-start = ((), (), s32[]{:S(2)}) async-start(), calls=%async_computation.3 | async-start | bytes 1048576 | tf_op jit(solution)/shard_map/psum | solution.py:300
Sparse Core Ops, SparseCore 0:
  50.5 47.0 reduce-scatter.1
Sparse Core Ops, SparseCore 1:
  56.6 133.0 all-reduce.3
  192.5 43.7 all-reduce.5
where the time goes:
time: 248 us; the launch traced here: 247 us
  waiting for transfers between devices  108 us (44%)
  blocking collectives  83.3 us (34%)
  Pallas kernels  22.3 us (9%)
  between operations  16.2 us (7%)
  local copies, waits for them, and re-layouts  7.46 us (3%)
  starting transfers between devices  6.99 us (3%)
    psum x1, blocking collectives, body(): small_out = lax.psum(small, ('dp', 'seq'))  76.1 us
    psum x1, waiting for transfers between devices, body(): query_out = lax.psum(share, 'dp')  46.6 us
    reduce_scatter x1, waiting for transfers between devices, body(): share = lax.psum_scatter(query, 'seq', scatter_dimension=1, tiled=True)  46.6 us
    psum x1, waiting for transfers between devices, body(): tab_out = lax.psum(tab, ('dp', 'seq'))  14.7 us
    pallas_call x1, Pallas kernels, body(): pl.pallas_call(forward_kernel, out_shape=(jax.ShapeDtypeStruct((rows, cha...  13.9 us
    pallas_call x1, Pallas kernels, body(): pl.pallas_call(backward_kernel, out_shape=(jax.ShapeDtypeStruct((chans, w...  8.33 us
    ppermute x1, starting transfers between devices, body(): lax.ppermute(ids[count - 3:], 'seq', up)  5.58 us
  transfers between devices with their start and end apart: 5, of which 3 were waited for; matrix products, arithmetic and copies ran while one was open for 2% of the time, Pallas kernels for 0%

commit v1 on v0

--- a/solution.py
+++ b/solution.py
@@ -303,9 +303,520 @@
     return (tab_out, small_out[0:3], small_out[3], small_out[4], query_out)
 
 
+MESH = pl.DeviceIdType.MESH
+BLOCK = 16
+TILE = 256
+
+
+def stacked(value):
+    hi = value.astype(BF16)
+    rest = value - hi.astype(F32)
+    mid = rest.astype(BF16)
+    low = (rest - mid.astype(F32)).astype(BF16)
+    return jnp.concatenate([hi.astype(F32), mid.astype(F32), low.astype(F32)], axis=0).astype(BF16)
+
+
+def packed_weights(start, total, rows):
+    n = lax.broadcasted_iota(jnp.int32, (8, rows), 0)
+    i = lax.broadcasted_iota(jnp.int32, (8, rows), 1)
+    b, p = n // 2, n % 2
+    even = (i % 2) == 0
+    r = (start + 2 * i + p) % 3
+    table = []
+    for o in OFFS:
+        at = start + 2 * i + o
+        inside = (at >= 0) & (at < total)
+        d = o - p
+        near = (d >= -2) & (d <= 2) & (r >= -d) & (r <= 2 - d)
+        w = jnp.where((b == 2) & near, 1.0 / 3.0, 0.0)
+        w = jnp.where((b == 0) & (p == o), 1.0, w)
+        if o in (0, 1):
+            w = jnp.where(b == 1, 0.5, w)
+            w = jnp.where(b == 3, 0.25, w)
+        else:
+            w = jnp.where((b == 3) & (even if o > 1 else ~even), 0.25, w)
+        table.append(jnp.where(inside, w, 0.0))
+    return table
+
+
+def over_blocks(value):
+    return value + pltpu.roll(value, 2, 0) + pltpu.roll(value, 4, 0) + pltpu.roll(value, 6, 0)
+
+
+def fused_kernel(
+    pad_ref, eo_ref, table_ref, cw_ref, sw_ref, gain_ref, wq_hbm, g_hbm,
+    tab_ref, small_ref, query_ref,
+    wq, g, tk, wt, wcat, pooled, ng, gb, pb, q, idm_s, w8_s, probs_s, hist, rr, lanes,
+    p_own, p_in, halo, x1_own, x1_in, x2_own, x2_in,
+    r1, s2, r2, zb, zr, own_z, tb, tr, ts, tz, sm, sz, sd,
+    in_sem, s_halo, r_halo, s_core, r_core, s_p1, r_p1, s_p2, r_p2, s_z, r_z, s_ag, r_ag,
+    s_t, r_t, s_sm, r_sm,
+):
+    d, s, t = lax.axis_index("dp"), lax.axis_index("seq"), lax.axis_index("tensor")
+    n_seq = lax.axis_size("seq")
+    x, y = d % 2, d // 2
+    x_near = y * 2 + (1 - x)
+    y_near = (1 - y) * 2 + x
+    corner = (1 - y) * 2 + (1 - x)
+    dp_peers = (x_near, y_near, corner)
+    seq_peers = [(s + e) % n_seq for e in range(1, n_seq)]
+    rows = eo_ref.shape[1]
+    vocab, chans = table_ref.shape
+    width = g.shape[1]
+    count = 2 * rows
+    total = count * n_seq
+    start = s * count
+    limit = total - pad_ref[0]
+    half, quarter, eighth = chans // 2, chans // 4, chans // 8
+    cols = width // n_seq
+    t_dp, t_seq = vocab // 4, vocab // 4 // n_seq
+
+    def remote(src, dst, send, recv, to):
+        return pltpu.make_async_remote_copy(
+            src_ref=src, dst_ref=dst, send_sem=send, recv_sem=recv,
+            device_id=to, device_id_type=MESH,
+        )
+
+    take_g = pltpu.make_async_copy(g_hbm, g, in_sem.at[0])
+    take_w = pltpu.make_async_copy(wq_hbm, wq, in_sem.at[1])
+    take_g.start()
+    take_w.start()
+
+    barrier = pltpu.get_barrier_semaphore()
+    peers = [(dd, s, t) for dd in dp_peers] + [(d, ss, t) for ss in seq_peers] + [(d, s, 1 - t)]
+    for peer in peers:
+        pl.semaphore_signal(barrier, inc=1, device_id=peer, device_id_type=MESH)
+
+    cs = cw_ref[...] * sw_ref[...]
+    p_own[...] = sum_parts(mm(stacked(pad8(cs)), table_ref[...], NT))
+    pl.semaphore_wait(barrier, len(peers))
+
+    put_p = remote(p_own, p_in, s_core.at[0], r_core.at[0], (d, s, 1 - t))
+    put_p.start()
+    edge = eo_ref.shape[0]
+    to_left = remote(
+        eo_ref.at[:, pl.ds(0, 128)], halo.at[1], s_halo.at[0], r_halo.at[1],
+        (d, jnp.maximum(s - 1, 0), t),
+    )
+    to_right = remote(
+        eo_ref.at[:, pl.ds(rows - 128, 128)], halo.at[0], s_halo.at[1], r_halo.at[0],
+        (d, jnp.minimum(s + 1, n_seq - 1), t),
+    )
+
+    @pl.when(s > 0)
+    def _():
+        to_left.start()
+
+    @pl.when(s < n_seq - 1)
+    def _():
+        to_right.start()
+
+    @pl.when(s == 0)
+    def _():
+        halo[0] = jnp.zeros((edge, 128), jnp.int32)
+
+    @pl.when(s == n_seq - 1)
+    def _():
+        halo[1] = jnp.zeros((edge, 128), jnp.int32)
+
+    for k in range(3):
+        def spell(c, carry, k=k):
+            at = pl.ds(pl.multiple_of(c * TILE, TILE), TILE)
+            tk[k * vocab : (k + 1) * vocab, at] = (
+                table_ref[:, at].astype(F32) * cw_ref[k : k + 1, at]
+            ).astype(BF16)
+            return carry
+
+        lax.fori_loop(0, chans // TILE, spell, 0)
+    take_g.wait()
+
+    def mask(c, carry):
+        at = pl.ds(pl.multiple_of(c * 64, 64), 64)
+        i = lax.broadcasted_iota(jnp.int32, (64, width), 0) + c * 64
+        g[at, :] = jnp.where(start + 2 * i < limit, g[at, :].astype(F32), 0.0).astype(BF16)
+        return carry
+
+    lax.fori_loop(0, rows // 64, mask, 0)
+
+    @pl.when(s > 0)
+    def _():
+        to_right.wait_recv()
+        to_left.wait_send()
+
+    @pl.when(s < n_seq - 1)
+    def _():
+        to_left.wait_recv()
+        to_right.wait_send()
+
+    put_p.wait()
+
+    wide = rows + 256
+    cat = jnp.concatenate([halo[0], eo_ref[...], halo[1]], axis=1)
+    lane = lax.broadcasted_iota(jnp.int32, cat.shape, 1)
+    row = lax.broadcasted_iota(jnp.int32, cat.shape, 0)
+    at_byte = start + 2 * (lane - 128) + row
+    cat = jnp.where((at_byte >= 0) & (at_byte < limit) & (row < 2), cat, -1)
+    core = slice(128, 128 + rows)
+    p3 = stacked(p_own[...] + p_in[...])
+    v_wide = lax.broadcasted_iota(jnp.int32, (vocab, wide), 0)
+
+    def picked(line):
+        hot = jnp.where(line == v_wide, 1.0, 0.0).astype(BF16)
+        return sum_parts(mm(p3, hot, NN))
+
+    even, odd = picked(cat[0:1]), picked(cat[1:2])
+    sc_even = pltpu.roll(odd, 1, 1)[0:1] + even[1:2] + odd[2:3]
+    sc_odd = even[0:1] + odd[1:2] + pltpu.roll(even, wide - 1, 1)[2:3]
+    se = jnp.broadcast_to(sc_even, (8, wide))
+    so = jnp.broadcast_to(sc_odd, (8, wide))
+    scores = [
+        pltpu.roll(se, 1, 1)[:, core], pltpu.roll(so, 1, 1)[:, core], se[:, core], so[:, core],
+        pltpu.roll(se, wide - 1, 1)[:, core], pltpu.roll(so, wide - 1, 1)[:, core],
+    ]
+    w8 = packed_weights(start, total, rows)
+    score = w8[0] * scores[0]
+    for n in range(1, 6):
+        score = score + w8[n] * scores[n]
+    expo = jnp.exp(score)
+    probs = expo / over_blocks(expo)
+    a = [0.5 * jnp.sum(probs * w, axis=0, keepdims=True) for w in w8]
+    probs_s[...] = probs
+    for n in range(6):
+        w8_s[n] = w8[n]
+    back = [pltpu.roll(cat, n, 1)[:, core] for n in (2, 1)]
+    fore = [pltpu.roll(cat, wide - n, 1)[:, core] for n in (1, 2)]
+    here = cat[:, core]
+    idm_s[...] = jnp.concatenate(
+        [back[0][1:2], back[1][0:2], here[0:2], fore[0][0:2], fore[1][0:1]], axis=0
+    )
+
+    def spread_in(n, carry):
+        at = pl.ds(pl.multiple_of(n * BLOCK, BLOCK), BLOCK)
+        v = lax.broadcasted_iota(jnp.int32, (BLOCK, rows), 0) + n * BLOCK
+        hits = [idm_s[j : j + 1, :] == v for j in range(8)]
+        for k in range(3):
+            acc = jnp.where(hits[k], a[0], 0.0)
+            for o in range(1, 6):
+                acc = acc + jnp.where(hits[o + k], a[o], 0.0)
+            wt[k, at, :] = acc.astype(BF16)
+        return carry
+
+    lax.fori_loop(0, vocab // BLOCK, spread_in, 0)
+    for k in range(3):
+        wcat[:, k * vocab : (k + 1) * vocab] = wt[k].astype(F32).T.astype(BF16)
+
+    lanes[...] = jnp.zeros_like(lanes)
+
+    def pool(c, carry):
+        at = pl.ds(pl.multiple_of(c * TILE, TILE), TILE)
+        part = mm(wcat[...], tk[:, at], NN)
+        pooled[:, at] = part
+        pb[:, at] = part.astype(BF16)
+        square = part * part
+        lanes[...] += square[:, 0:128] + square[:, 128:256]
+        return carry
+
+    lax.fori_loop(0, chans // TILE, pool, 0)
+    x1_own[...] = jnp.broadcast_to(jnp.sum(lanes[...].T, axis=0, keepdims=True), (8, rows))
+    put_1 = remote(x1_own, x1_in, s_core.at[1], r_core.at[1], (d, s, 1 - t))
+    put_1.start()
+    put_1.wait()
+    scale = lax.rsqrt((x1_own[...] + x1_in[...]) / D + EPS)
+    scale_c = scale.T[:, 0:1]
+
+    def product(at_row):
+        at = pl.ds(pl.multiple_of(at_row, 128), quarter)
+        normed = (pooled[:, at] * scale_c * gain_ref[:, at]).astype(BF16)
+        q[at, :] = mm(normed, g[...], TN).astype(BF16)
+
+    bit1, bit2 = (x, y), (y, x)
+    near1 = ((x_near, s, t), (y_near, s, t))
+    near2 = ((y_near, s, t), (x_near, s, t))
+
+    def q_rows(h, first, second):
+        return pl.ds(pl.multiple_of(h * half + first * quarter + second * eighth, eighth), eighth)
+
+    p1 = {}
+    for h in range(2):
+        product(h * half + (1 - bit1[h]) * quarter)
+        for part in range(2):
+            second = bit2[h] if part else 1 - bit2[h]
+            p1[h, part] = remote(
+                q.at[q_rows(h, 1 - bit1[h], second)], r1.at[h, part],
+                s_p1.at[h, part], r_p1.at[h, part], near1[h],
+            )
+            p1[h, part].start()
+    for h in range(2):
+        product(h * half + bit1[h] * quarter)
+
+    take_w.wait()
+    lanes[...] = jnp.zeros_like(lanes)
+
+    def pull_back(c, carry):
+        at = pl.ds(pl.multiple_of(c * TILE, TILE), TILE)
+        part = mm(g[...], wq[at, :], NT)
+        ng[:, at] = part
+        gained = part * gain_ref[:, at]
+        gb[:, at] = gained.astype(BF16)
+        inner = pooled[:, at] * gained
+        lanes[...] += inner[:, 0:128] + inner[:, 128:256]
+        return carry
+
+    lax.fori_loop(0, chans // TILE, pull_back, 0)
+    found = []
+    for source in (gb, pb):
+        sums = tuple(jnp.zeros((8, rows), F32) for o in range(6))
+        for k in range(3):
+            rr[...] = mm(tk[k * vocab : (k + 1) * vocab, :], source[...], NT)
+
+            def select(n, accs, k=k):
+                line = rr[pl.ds(pl.multiple_of(n * 8, 8), 8), :]
+                v = lax.broadcasted_iota(jnp.int32, (8, rows), 0) + n * 8
+                return tuple(
+                    accs[o] + jnp.where(idm_s[o + k : o + k + 1, :] == v, line, 0.0)
+                    for o in range(6)
+                )
+
+            sums = lax.fori_loop(0, vocab // 8, select, sums)
+        found += [jnp.sum(acc, axis=0, keepdims=True) for acc in sums]
+    found.append(jnp.sum(lanes[...].T, axis=0, keepdims=True))
+    found.append(jnp.zeros((3, rows), F32))
+    x2_own[...] = jnp.concatenate(found, axis=0)
+    put_2 = remote(x2_own, x2_in, s_core.at[2], r_core.at[2], (d, s, 1 - t))
+    put_2.start()
+
+    p2 = {}
+    for h in range(2):
+        p1[h, 0].wait_recv()
+        rows_h = q_rows(h, bit1[h], 1 - bit2[h])
+        s2[h] = (q[rows_h, :].astype(F32) + r1[h, 0].astype(F32)).astype(BF16)
+        for e in range(n_seq):
+            at = pl.ds(pl.multiple_of((s + e + 1) % n_seq * cols, 128), cols)
+            p2[h, e] = remote(
+                s2.at[h, :, at], r2.at[h, :, at], s_p2.at[h, e], r_p2.at[h, e], near2[h]
+            )
+            p2[h, e].start()
+
+    put_2.wait()
+    sums = x2_own[...] + x2_in[...]
+    pull = scale[0:1] * scale[0:1] * scale[0:1] * (sums[12:13] / D)
+    w8 = [w8_s[n] for n in range(6)]
+    probs = probs_s[...]
+    pgrad = None
+    for o in range(6):
+        term = w8[o] * (scale[0:1] * sums[o : o + 1] - pull * sums[o + 6 : o + 7])
+        pgrad = term if pgrad is None else pgrad + term
+    pgrad = 0.5 * pgrad
+    sgrad = probs * (pgrad - over_blocks(probs * pgrad))
+    ds = [jnp.sum(sgrad * w, axis=0, keepdims=True) for w in w8]
+
+    def count_in(n, carry):
+        at = pl.ds(pl.multiple_of(n * BLOCK, BLOCK), BLOCK)
+        v = lax.broadcasted_iota(jnp.int32, (BLOCK, rows), 0) + n * BLOCK
+        hits = [idm_s[j : j + 1, :] == v for j in range(8)]
+        for k in range(3):
+            acc = jnp.where(hits[k], ds[0], 0.0)
+            for o in range(1, 6):
+                acc = acc + jnp.where(hits[o + k], ds[o], 0.0)
+            hist[k, at, :] = jnp.broadcast_to(jnp.sum(acc, axis=1, keepdims=True), (BLOCK, 128))
+        return carry
+
+    lax.fori_loop(0, vocab // BLOCK, count_in, 0)
+    pull_c = jnp.broadcast_to(pull, (8, rows)).T[:, 0:1]
+
+    def table_step(c, carry):
+        at = pl.ds(pl.multiple_of(c * TILE, TILE), TILE)
+        tab = table_ref[:, at].astype(F32)
+        cw, sw, gain = cw_ref[:, at], sw_ref[:, at], gain_ref[:, at]
+        ngc, pc = ng[:, at], pooled[:, at]
+        scaled = ngc * scale_c
+        gain_term = jnp.sum(scaled * pc, axis=0, keepdims=True)
+        pg = (scaled * gain - pull_c * pc).astype(BF16)
+        whole, outs, score = None, [], None
+        for k in range(3):
+            hist_k = hist[k][:, 0:1]
+            full = mm(wt[k], pg, NN) + hist_k * sw
+            term = cw[k : k + 1] * full
+            whole = term if whole is None else whole + term
+            outs.append(jnp.sum(full * tab, axis=0, keepdims=True))
+            term = cw[k : k + 1] * jnp.sum(hist_k * tab, axis=0, keepdims=True)
+            score = term if score is None else score + term
+        tb[:, at] = whole.astype(BF16)
+        sm[:, at] = jnp.concatenate(outs + [score, gain_term, jnp.zeros((3, TILE), F32)], axis=0)
+        return carry
+
+    lax.fori_loop(0, chans // TILE, table_step, 0)
+
+    t_rs, sm_z = [], []
+    for e, dd in enumerate(dp_peers):
+        block = tb.at[pl.ds(pl.multiple_of(dd * t_dp, t_dp), t_dp)]
+        t_rs.append(remote(block, tr.at[d], s_t.at[e], r_t.at[e], (dd, s, t)))
+        t_rs[-1].start()
+    for e, ss in enumerate(seq_peers):
+        sm_z.append(remote(sm, sz.at[s], s_sm.at[e], r_sm.at[e], (d, ss, t)))
+        sm_z[-1].start()
+    tr[d] = tb[pl.ds(pl.multiple_of(d * t_dp, t_dp), t_dp), :]
+    sz[s] = sm[...]
+
+    for h in range(2):
+        p1[h, 1].wait_recv()
+    q_z = {}
+    for e in range(n_seq):
+        j = (s + e + 1) % n_seq
+        at = pl.ds(pl.multiple_of(j * cols, 128), cols)
+        for h in range(2):
+            p2[h, e].wait_recv()
+            rows_h = q_rows(h, bit1[h], bit2[h])
+            block = q[rows_h, at].astype(F32) + r1[h, 1, :, at].astype(F32)
+            block = block + r2[h, :, at].astype(F32)
+            if e < n_seq - 1:
+                zb[h, e] = block.astype(BF16)
+                q_z[h, e] = remote(
+                    zb.at[h, e], zr.at[h, e], s_z.at[h, e], r_z.at[h, e], (d, j, t)
+                )
+                q_z[h, e].start()
+            else:
+                own_z[h] = block
+
+    for copy in t_rs:
+        copy.wait_recv()
+    acc = tr[0].astype(F32)
+    for n in range(1, 4):
+        acc = acc + tr[n].astype(F32)
+    ts[...] = acc.astype(BF16)
+    t_z = []
+    for e, ss in enumerate(seq_peers):
+        block = ts.at[pl.ds(pl.multiple_of(ss * t_seq, t_seq), t_seq)]
+        t_z.append(remote(block, tz.at[s], s_t.at[3 + e], r_t.at[3 + e], (d, ss, t)))
+        t_z[-1].start()
+    tz[s] = ts[pl.ds(pl.multiple_of(s * t_seq, t_seq), t_seq), :]
+
+    for copy in sm_z:
+        copy.wait_recv()
+    acc = sz[0]
+    for n in range(1, n_seq):
+        acc = acc + sz[n]
+    sd[d] = acc
+    sm_d = []
+    for e, dd in enumerate(dp_peers):
+        sm_d.append(remote(sd.at[d], sd.at[d], s_sm.at[3 + e], r_sm.at[3 + e], (dd, s, t)))
+        sm_d[-1].start()
+
+    q_ag = []
+    for h in range(2):
+        block = own_z[h]
+        for e in range(n_seq - 1):
+            q_z[h, e].wait_recv()
+            block = block + zr[h, e].astype(F32)
+        mine = q_rows(h, bit1[h], bit2[h])
+        query_ref[mine, :] = block.astype(BF16)
+        for e, dd in enumerate(dp_peers):
+            q_ag.append(
+                remote(
+                    query_ref.at[mine], query_ref.at[mine], s_ag.at[h, e], r_ag.at[h, e], (dd, s, t)
+                )
+            )
+            q_ag[-1].start()
+
+    for copy in t_z:
+        copy.wait_recv()
+    acc = tz[0].astype(F32)
+    for n in range(1, n_seq):
+        acc = acc + tz[n].astype(F32)
+    mine = pl.ds(pl.multiple_of(d * t_dp + s * t_seq, t_seq), t_seq)
+    tab_ref[mine, :] = acc.astype(BF16)
+    t_back = []
+    for e, ss in enumerate(seq_peers):
+        t_back.append(
+            remote(tab_ref.at[mine], tab_ref.at[mine], s_t.at[6 + e], r_t.at[6 + e], (d, ss, t))
+        )
+        t_back[-1].start()
+    for copy in t_back:
+        copy.wait_recv()
+    t_ag = []
+    mine = pl.ds(pl.multiple_of(d * t_dp, t_dp), t_dp)
+    for e, dd in enumerate(dp_peers):
+        t_ag.append(
+            remote(tab_ref.at[mine], tab_ref.at[mine], s_t.at[9 + e], r_t.at[9 + e], (dd, s, t))
+        )
+        t_ag[-1].start()
+
+    for copy in sm_d:
+        copy.wait_recv()
+    small_ref[...] = (sd[0] + sd[1]) + (sd[2] + sd[3])
+    for copy in q_ag + t_ag:
+        copy.wait_recv()
+    started = list(p1.values()) + list(p2.values()) + list(q_z.values())
+    for copy in started + t_rs + t_z + t_back + t_ag + sm_z + sm_d + q_ag:
+        copy.wait_send()
+
+
+def pad8(value):
+    return jnp.concatenate([value, jnp.zeros((8 - value.shape[0], value.shape[1]), F32)], axis=0)
+
+
+def sum_parts(value):
+    return value[0:8] + value[8:16] + value[16:24]
+
+
+def fused_body(
+    byte_ids, pad_lengths, table, conv_weight, score_weight, norm_gain, query_weight, query_grad
+):
+    count = byte_ids.shape[1]
+    rows = count // 2
+    vocab, chans = table.shape
+    width = query_grad.shape[2]
+    n_seq = lax.axis_size("seq")
+    cols = width // n_seq
+    part, t_dp = chans // 8, vocab // 4
+    eo = jnp.pad(byte_ids[0].reshape(rows, 2).T, ((0, 6), (0, 0)))
+    vm = pl.BlockSpec(memory_space=pltpu.VMEM)
+    sm = pl.BlockSpec(memory_space=pltpu.SMEM)
+    hbm = pl.BlockSpec(memory_space=pl.ANY)
+    V, DMA = pltpu.VMEM, pltpu.SemaphoreType.DMA
+    tab, small, query = pl.pallas_call(
+        fused_kernel,
+        out_shape=(
+            jax.ShapeDtypeStruct((vocab, chans), BF16),
+            jax.ShapeDtypeStruct((8, chans), F32),
+            jax.ShapeDtypeStruct((chans, cols), BF16),
+        ),
+        in_specs=[sm] + [vm] * 5 + [hbm] * 2,
+        out_specs=(vm,) * 3,
+        scratch_shapes=[
+            V((chans, width), BF16), V((rows, width), BF16), V((3 * vocab, chans), BF16),
+            V((3, vocab, rows), BF16), V((rows, 3 * vocab), BF16), V((rows, chans), F32),
+            V((rows, chans), F32), V((rows, chans), BF16), V((rows, chans), BF16),
+            V((chans, width), BF16), V((8, rows), jnp.int32), V((6, 8, rows), F32),
+            V((8, rows), F32), V((3, vocab, 128), F32), V((vocab, rows), F32), V((rows, 128), F32),
+            V((8, vocab), F32), V((8, vocab), F32), V((2, 8, 128), jnp.int32),
+            V((8, rows), F32), V((8, rows), F32), V((16, rows), F32), V((16, rows), F32),
+            V((2, 2, part, width), BF16), V((2, part, width), BF16), V((2, part, width), BF16),
+            V((2, n_seq - 1, part, cols), BF16), V((2, n_seq - 1, part, cols), BF16),
+            V((2, part, cols), F32), V((vocab, chans), BF16), V((4, t_dp, chans), BF16),
+            V((t_dp, chans), BF16), V((n_seq, t_dp // n_seq, chans), BF16),
+            V((8, chans), F32), V((n_seq, 8, chans), F32), V((4, 8, chans), F32),
+            DMA((2,)), DMA((2,)), DMA((2,)), DMA((3,)), DMA((3,)),
+            DMA((2, 2)), DMA((2, 2)), DMA((2, n_seq)), DMA((2, n_seq)),
+            DMA((2, n_seq - 1)), DMA((2, n_seq - 1)), DMA((2, 3)), DMA((2, 3)),
+            DMA((12,)), DMA((12,)), DMA((6,)), DMA((6,)),
+        ],
+        compiler_params=pltpu.CompilerParams(collective_id=0, has_side_effects=True),
+        name="fused",
+    )(
+        pad_lengths, eo, table, conv_weight, score_weight[None, :], norm_gain[None, :],
+        query_weight, query_grad[0],
+    )
+    return (tab, small[0:3], small[3], small[4], query)
+
+
+def fits(mesh):
+    return mesh.shape["dp"] == 4 and mesh.shape["seq"] == 4 and mesh.shape["tensor"] == 2
+
+
 def solution(mesh):
     return jax.shard_map(
-        body,
+        fused_body if fits(mesh) else body,
         mesh=mesh,
         in_specs=(
             P("dp", "seq"),

time: 248 us -> 73.5 us (0.30)
  waiting for transfers between devices: 108 us -> 0 us
  blocking collectives: 83.3 us -> 0 us
  Pallas kernels: 22.3 us -> 62.4 us
  between operations: 16.2 us -> 1.3 us
  starting transfers between devices: 6.99 us -> 0 us
    psum x3 -> x0, blocking collectives: 83.3 us -> none  [the longest x1 76.1 us: body(): small_out = lax.psum(small, ('dp', 'seq'))]
    psum x2 -> x0, waiting for transfers between devices: 61.3 us -> none  [the longest x1 46.6 us: body(): query_out = lax.psum(share, 'dp')]
    reduce_scatter x1 -> x0, waiting for transfers between devices: 46.6 us -> none  [body(): share = lax.psum_scatter(query, 'seq', scatter_dimension=1, tiled=True)]
    pallas_call x2 -> x1, Pallas kernels: 22.3 us -> 62.4 us  [fused_body(): pl.pallas_call(fused_kernel, out_shape=(jax.ShapeDtypeStruct((vocab, chan...]
    ppermute x2 -> x0, starting transfers between devices: 6.86 us -> none  [the longest x1 5.58 us: body(): lax.ppermute(ids[count - 3:], 'seq', up)]
  transfers between devices with their start and end apart: 5 -> 0, of which waited for: 3 -> 0; matrix products, arithmetic and copies ran while one was open for 2% -> 0% of each run, Pallas kernels for 0% -> 0%
where the time goes in v1:
time: 73.5 us; the launch traced here: 73.1 us
  Pallas kernels  62.4 us (85%)
  local copies, waits for them, and re-layouts  7.98 us (11%)
  other arithmetic  1.35 us (2%)
  between operations  1.3 us (2%)
    pallas_call x1, Pallas kernels, fused_body(): pl.pallas_call(fused_kernel, out_shape=(jax.ShapeDtypeStruct((vocab, chan...  62.4 us
    unnamed x3, local copies, waits for them, and re-layouts  4.25 us
    slice x2, local copies, waits for them, and re-layouts, fused_body(): return (tab, small[0:3], small[3], small[4], query)  2.8 us

profile of v1, /device:TPU:0, one launch (start us, length us, event | category | flops | bytes accessed | tf_op | source)
XLA Modules:
  0.0 73.1 jit_solution(13215357389808941435)
XLA Ops:
  0.6 0.5 broadcast.5
  1.1 1.3 %reduce.3 = s32[1024]{0:T(1024)S(1)} reduce(s32[1,1024]{1,0:T(1,128)} %param.8, s32[]{:T(128)} %broadcast.5), dimensions={0}, to_apply=%param.8.reduce_sub_computation.3 | reduce | bytes 8196 | tf_op args[0]
  2.5 0.2 reshape_squeeze.3
  2.7 0.1 copy.13
  2.8 0.6 pad.4.eo_ref
  4.1 62.4 %fused.1 = (bf16[256,1024]{1,0:T(8,128)(2,1)}, f32[8,1024]{1,0:T(8,128)}, bf16[1024,256]{1,0:T(8,128)(2,1)}) custom-call(s32[1]{0:T(128)S(6)} %copy.16.pad_ref, s32[8,512]{1,0:T(8,128)} %pad.4.eo_ref, bf16[256,1024]{1,0:T(8,128)(2,1)} %table_ref.1, f32[3,1024]{1,0:T(4,128)} %cw_ref.1, f32[1,1024]{1,0:T(1,128)} %bitcast.10, f32[1,1024]{1,0:T(1,128)} %bitcast.11, ...), custom_call_target="tpu_custom_call" | custom-call | tf_op jit(solution)/shard_map/fused/pallas_call | solution.py:777
  66.5 1.4 %fusion = (f32[1,1024]{1,0:T(1,128)}, f32[1,1024]{1,0:T(1,128)}) fusion(f32[8,1024]{1,0:T(8,128)} %get-tuple-element.9), kind=kLoop, calls=%fused_computation | loop fusion | bytes 16384 | tf_op jit(solution)/shard_map/slice | solution.py:810
  68.0 1.4 %slice.9 = f32[3,1024]{1,0:T(4,128)} slice(f32[8,1024]{1,0:T(8,128)} %get-tuple-element.9), slice={[0:3], [0:1024]} | slice | bytes 24576 | tf_op jit(solution)/shard_map/slice | solution.py:810
  69.3 1.9 %copy.17 = bf16[256,1024]{1,0:T(8,128)(2,1)} copy(bf16[256,1024]{1,0:T(8,128)(2,1)} %get-tuple-element.18) | data formatting | bytes 1048576
  71.2 1.9 %copy.18 = bf16[1024,256]{1,0:T(8,128)(2,1)} copy(bf16[1024,256]{1,0:T(8,128)(2,1)} %get-tuple-element.22) | data formatting | bytes 1048576

commit v2 on v1

--- a/solution.py
+++ b/solution.py
@@ -344,7 +344,7 @@
 
 
 def fused_kernel(
-    pad_ref, eo_ref, table_ref, cw_ref, sw_ref, gain_ref, wq_hbm, g_hbm,
+    pad_ref, ids_ref, table_ref, cw_ref, sw_ref, gain_ref, wq_hbm, g_hbm,
     tab_ref, small_ref, query_ref,
     wq, g, tk, wt, wcat, pooled, ng, gb, pb, q, idm_s, w8_s, probs_s, hist, rr, lanes,
     p_own, p_in, halo, x1_own, x1_in, x2_own, x2_in,
@@ -360,10 +360,10 @@
     corner = (1 - y) * 2 + (1 - x)
     dp_peers = (x_near, y_near, corner)
     seq_peers = [(s + e) % n_seq for e in range(1, n_seq)]
-    rows = eo_ref.shape[1]
+    count = ids_ref.shape[1]
+    rows = count // 2
     vocab, chans = table_ref.shape
     width = g.shape[1]
-    count = 2 * rows
     total = count * n_seq
     start = s * count
     limit = total - pad_ref[0]
@@ -393,13 +393,12 @@
 
     put_p = remote(p_own, p_in, s_core.at[0], r_core.at[0], (d, s, 1 - t))
     put_p.start()
-    edge = eo_ref.shape[0]
     to_left = remote(
-        eo_ref.at[:, pl.ds(0, 128)], halo.at[1], s_halo.at[0], r_halo.at[1],
+        ids_ref.at[:, pl.ds(0, 128)], halo.at[1], s_halo.at[0], r_halo.at[1],
         (d, jnp.maximum(s - 1, 0), t),
     )
     to_right = remote(
-        eo_ref.at[:, pl.ds(rows - 128, 128)], halo.at[0], s_halo.at[1], r_halo.at[0],
+        ids_ref.at[:, pl.ds(count - 128, 128)], halo.at[0], s_halo.at[1], r_halo.at[0],
         (d, jnp.minimum(s + 1, n_seq - 1), t),
     )
 
@@ -413,11 +412,11 @@
 
     @pl.when(s == 0)
     def _():
-        halo[0] = jnp.zeros((edge, 128), jnp.int32)
+        halo[0] = jnp.zeros((1, 128), jnp.int32)
 
     @pl.when(s == n_seq - 1)
     def _():
-        halo[1] = jnp.zeros((edge, 128), jnp.int32)
+        halo[1] = jnp.zeros((1, 128), jnp.int32)
 
     for k in range(3):
         def spell(c, carry, k=k):
@@ -450,13 +449,34 @@
 
     put_p.wait()
 
-    wide = rows + 256
-    cat = jnp.concatenate([halo[0], eo_ref[...], halo[1]], axis=1)
+    wide = rows + 128
+    line = jnp.concatenate([halo[0], ids_ref[...], halo[1]], axis=1).astype(F32)
+    pieces = wide // 128
+    line = jnp.concatenate(
+        [line[:, n * 256 : (n + 1) * 256] for n in range(pieces)]
+        + [jnp.zeros((8 - pieces % 8, 256), F32)] * (pieces % 8 > 0),
+        axis=0,
+    )
+    r = lax.broadcasted_iota(jnp.int32, (256, 256), 0)
+    c = lax.broadcasted_iota(jnp.int32, (256, 256), 1)
+    sift = jnp.where(r == jnp.where(c < 128, 2 * c, 2 * c - 255), 1.0, 0.0).astype(BF16)
+    sifted = mm(line.astype(BF16), sift, NN)
+    cat = jnp.concatenate(
+        [
+            jnp.concatenate([sifted[n : n + 1, p * 128 : (p + 1) * 128] for n in range(pieces)], axis=1)
+            for p in range(2)
+        ]
+        + [jnp.zeros((6, wide), F32)],
+        axis=0,
+    ).astype(jnp.int32)
     lane = lax.broadcasted_iota(jnp.int32, cat.shape, 1)
     row = lax.broadcasted_iota(jnp.int32, cat.shape, 0)
-    at_byte = start + 2 * (lane - 128) + row
+    at_byte = start + 2 * (lane - 64) + row
     cat = jnp.where((at_byte >= 0) & (at_byte < limit) & (row < 2), cat, -1)
-    core = slice(128, 128 + rows)
+
+    def shifted(value, n):
+        return pltpu.roll(value, wide - 64 - n, 1)[:, 0:rows]
+
     p3 = stacked(p_own[...] + p_in[...])
     v_wide = lax.broadcasted_iota(jnp.int32, (vocab, wide), 0)
 
@@ -469,10 +489,7 @@
     sc_odd = even[0:1] + odd[1:2] + pltpu.roll(even, wide - 1, 1)[2:3]
     se = jnp.broadcast_to(sc_even, (8, wide))
     so = jnp.broadcast_to(sc_odd, (8, wide))
-    scores = [
-        pltpu.roll(se, 1, 1)[:, core], pltpu.roll(so, 1, 1)[:, core], se[:, core], so[:, core],
-        pltpu.roll(se, wide - 1, 1)[:, core], pltpu.roll(so, wide - 1, 1)[:, core],
-    ]
+    scores = [shifted(value, n) for n in (-1, 0, 1) for value in (se, so)]
     w8 = packed_weights(start, total, rows)
     score = w8[0] * scores[0]
     for n in range(1, 6):
@@ -483,11 +500,9 @@
     probs_s[...] = probs
     for n in range(6):
         w8_s[n] = w8[n]
-    back = [pltpu.roll(cat, n, 1)[:, core] for n in (2, 1)]
-    fore = [pltpu.roll(cat, wide - n, 1)[:, core] for n in (1, 2)]
-    here = cat[:, core]
+    near = [shifted(cat, n) for n in (-2, -1, 0, 1, 2)]
     idm_s[...] = jnp.concatenate(
-        [back[0][1:2], back[1][0:2], here[0:2], fore[0][0:2], fore[1][0:1]], axis=0
+        [near[0][1:2], near[1][0:2], near[2][0:2], near[3][0:2], near[4][0:1]], axis=0
     )
 
     def spread_in(n, carry):
@@ -751,6 +766,14 @@
         copy.wait_send()
 
 
+def finish_kernel(tab_ref, small_ref, query_ref, tab_out, conv_out, score_out, gain_out, query_out):
+    conv_out[...] = small_ref[0:3]
+    score_out[...] = small_ref[3:4]
+    gain_out[...] = small_ref[4:5]
+    tab_out[...] = tab_ref[...]
+    query_out[...] = query_ref[...]
+
+
 def pad8(value):
     return jnp.concatenate([value, jnp.zeros((8 - value.shape[0], value.shape[1]), F32)], axis=0)
 
@@ -769,7 +792,6 @@
     n_seq = lax.axis_size("seq")
     cols = width // n_seq
     part, t_dp = chans // 8, vocab // 4
-    eo = jnp.pad(byte_ids[0].reshape(rows, 2).T, ((0, 6), (0, 0)))
     vm = pl.BlockSpec(memory_space=pltpu.VMEM)
     sm = pl.BlockSpec(memory_space=pltpu.SMEM)
     hbm = pl.BlockSpec(memory_space=pl.ANY)
@@ -789,7 +811,7 @@
             V((rows, chans), F32), V((rows, chans), BF16), V((rows, chans), BF16),
             V((chans, width), BF16), V((8, rows), jnp.int32), V((6, 8, rows), F32),
             V((8, rows), F32), V((3, vocab, 128), F32), V((vocab, rows), F32), V((rows, 128), F32),
-            V((8, vocab), F32), V((8, vocab), F32), V((2, 8, 128), jnp.int32),
+            V((8, vocab), F32), V((8, vocab), F32), V((2, 1, 128), jnp.int32),
             V((8, rows), F32), V((8, rows), F32), V((16, rows), F32), V((16, rows), F32),
             V((2, 2, part, width), BF16), V((2, part, width), BF16), V((2, part, width), BF16),
             V((2, n_seq - 1, part, cols), BF16), V((2, n_seq - 1, part, cols), BF16),
@@ -804,10 +826,27 @@
         compiler_params=pltpu.CompilerParams(collective_id=0, has_side_effects=True),
         name="fused",
     )(
-        pad_lengths, eo, table, conv_weight, score_weight[None, :], norm_gain[None, :],
+        pad_lengths, byte_ids, table, conv_weight, score_weight[None, :], norm_gain[None, :],
         query_weight, query_grad[0],
     )
-    return (tab, small[0:3], small[3], small[4], query)
+    return pl.pallas_call(
+        finish_kernel,
+        out_shape=(
+            jax.ShapeDtypeStruct((vocab, chans), BF16),
+            jax.ShapeDtypeStruct((3, chans), F32),
+            jax.ShapeDtypeStruct((1, chans), F32),
+            jax.ShapeDtypeStruct((1, chans), F32),
+            jax.ShapeDtypeStruct((chans, cols), BF16),
+        ),
+        in_specs=[vm] * 3,
+        out_specs=(vm,) * 5,
+        name="finish",
+    )(tab, small, query)
+
+
+def fused_outer(*args):
+    tab, conv, score, gain, query = fused_body(*args)
+    return (tab, conv, score.reshape(-1), gain.reshape(-1), query)
 
 
 def fits(mesh):
@@ -816,7 +855,7 @@
 
 def solution(mesh):
     return jax.shard_map(
-        fused_body if fits(mesh) else body,
+        fused_outer if fits(mesh) else body,
         mesh=mesh,
         in_specs=(
             P("dp", "seq"),

time: 73.5 us -> 66.2 us (0.901)
  local copies, waits for them, and re-layouts: 7.98 us -> 0 us
  Pallas kernels: 62.4 us -> 64.8 us
  other arithmetic: 1.35 us -> 0 us
    unnamed x3 -> x0, local copies, waits for them, and re-layouts: 4.25 us -> none
    slice x2 -> x0, local copies, waits for them, and re-layouts: 2.8 us -> none  [fused_body(): return (tab, small[0:3], small[3], small[4], query)]
    pallas_call x0 -> x1, Pallas kernels: none -> 2.23 us  [fused_body(): pl.pallas_call(finish_kernel, out_shape=(jax.ShapeDtypeStruct((vocab, cha...]
    unnamed x1 -> x0, other arithmetic: 1.35 us -> none
where the time goes in v2:
time: 66.2 us; the launch traced here: 66.1 us
  Pallas kernels  64.8 us (98%)
  between operations  1.29 us (2%)
    pallas_call x1, Pallas kernels, fused_body(): pl.pallas_call(fused_kernel, out_shape=(jax.ShapeDtypeStruct((vocab, chan...  62.5 us
    pallas_call x1, Pallas kernels, fused_body(): pl.pallas_call(finish_kernel, out_shape=(jax.ShapeDtypeStruct((vocab, cha...  2.23 us

profile of v2, /device:TPU:0, one launch (start us, length us, event | category | flops | bytes accessed | tf_op | source)
XLA Modules:
  0.0 66.1 jit_solution(12946008356476422523)
XLA Ops:
  1.3 62.5 %fused.1 = (bf16[256,1024]{1,0:T(8,128)(2,1)}, f32[8,1024]{1,0:T(8,128)}, bf16[1024,256]{1,0:T(8,128)(2,1)}) custom-call(s32[1]{0:T(128)S(6)} %copy.13.pad_ref, s32[1,1024]{1,0:T(1,128)} %ids_ref.1, bf16[256,1024]{1,0:T(8,128)(2,1)} %table_ref.1, f32[3,1024]{1,0:T(4,128)} %cw_ref.1, f32[1,1024]{1,0:T(1,128)} %bitcast.6, f32[1,1024]{1,0:T(1,128)} %bitcast.7, ...), custom_call_target="tpu_custom_call" | custom-call | tf_op jit(solution)/shard_map/fused/pallas_call | solution.py:799
  63.8 2.2 %finish.1 = (bf16[256,1024]{1,0:T(8,128)(2,1)}, f32[3,1024]{1,0:T(4,128)}, f32[1,1024]{1,0:T(1,128)}, f32[1,1024]{1,0:T(1,128)}, bf16[1024,256]{1,0:T(8,128)(2,1)}) custom-call(bf16[256,1024]{1,0:T(8,128)(2,1)} %get-tuple-element.13.tab_ref, f32[8,1024]{1,0:T(8,128)} %get-tuple-element.14.small_ref, bf16[1024,256]{1,0:T(8,128)(2,1)} %get-tuple-element.15.query_ref), custom_call_target="tpu_custom_call" | custom-call | tf_op jit(solution)/shard_map/finish/pallas_call | solution.py:832

commit v3 on v2

--- a/solution.py
+++ b/solution.py
@@ -346,11 +346,11 @@
 def fused_kernel(
     pad_ref, ids_ref, table_ref, cw_ref, sw_ref, gain_ref, wq_hbm, g_hbm,
     tab_ref, small_ref, query_ref,
-    wq, g, tk, wt, wcat, pooled, ng, gb, pb, q, idm_s, w8_s, probs_s, hist, rr, lanes,
+    wq, g, tk, wt, wcat, pooled, ng, gb, pb, q, idm_s, a_s, w8_s, probs_s, hist, rr, lanes,
     p_own, p_in, halo, x1_own, x1_in, x2_own, x2_in,
-    r1, s2, r2, zb, zr, own_z, tb, tr, ts, tz, sm, sz, sd,
+    r1, s2, r2, zb, zr, own_z, zq, zs, zd, tb, tr, ts, tz, own_t, sm, sz, sd,
     in_sem, s_halo, r_halo, s_core, r_core, s_p1, r_p1, s_p2, r_p2, s_z, r_z, s_ag, r_ag,
-    s_t, r_t, s_sm, r_sm,
+    s_zq, r_zq, s_zd, r_zd, s_trs, r_trs, s_tz, r_tz, s_tb, r_tb, s_ta, r_ta, s_sm, r_sm,
 ):
     d, s, t = lax.axis_index("dp"), lax.axis_index("seq"), lax.axis_index("tensor")
     n_seq = lax.axis_size("seq")
@@ -367,7 +367,9 @@
     total = count * n_seq
     start = s * count
     limit = total - pad_ref[0]
-    half, quarter, eighth = chans // 2, chans // 4, chans // 8
+    first_z = 3 * chans // 4
+    half, quarter, eighth = first_z // 2, first_z // 4, first_z // 8
+    step_z = (chans - first_z) // 4
     cols = width // n_seq
     t_dp, t_seq = vocab // 4, vocab // 4 // n_seq
 
@@ -436,6 +438,17 @@
         return carry
 
     lax.fori_loop(0, rows // 64, mask, 0)
+    take_w.wait()
+
+    def pull_back(c, carry):
+        at = pl.ds(pl.multiple_of(c * TILE, TILE), TILE)
+        part = mm(g[...], wq[at, :], NT)
+        ng[:, at] = part
+        gb[:, at] = (part * gain_ref[:, at]).astype(BF16)
+        return carry
+
+    split_at = chans // TILE // 2
+    lax.fori_loop(0, split_at, pull_back, 0)
 
     @pl.when(s > 0)
     def _():
@@ -501,19 +514,29 @@
     for n in range(6):
         w8_s[n] = w8[n]
     near = [shifted(cat, n) for n in (-2, -1, 0, 1, 2)]
-    idm_s[...] = jnp.concatenate(
-        [near[0][1:2], near[1][0:2], near[2][0:2], near[3][0:2], near[4][0:1]], axis=0
-    )
+    idm = [near[0][1:2], near[1][0:1], near[1][1:2], near[2][0:1], near[2][1:2],
+           near[3][0:1], near[3][1:2], near[4][0:1]]
+    for j in range(8):
+        idm_s[j] = jnp.broadcast_to(idm[j], (8, rows))
+    for o in range(6):
+        a_s[o] = jnp.broadcast_to(a[o], (8, rows))
+
+    def spread_rows(n):
+        v = lax.broadcasted_iota(jnp.int32, (8, rows), 0) + n
+        hits = [idm_s[j] == v for j in range(8)]
+        accs = []
+        for k in range(3):
+            acc = jnp.where(hits[k], a_s[0], 0.0)
+            for o in range(1, 6):
+                acc = acc + jnp.where(hits[o + k], a_s[o], 0.0)
+            accs.append(acc)
+        return accs
 
     def spread_in(n, carry):
         at = pl.ds(pl.multiple_of(n * BLOCK, BLOCK), BLOCK)
-        v = lax.broadcasted_iota(jnp.int32, (BLOCK, rows), 0) + n * BLOCK
-        hits = [idm_s[j : j + 1, :] == v for j in range(8)]
+        top, low = spread_rows(n * BLOCK), spread_rows(n * BLOCK + 8)
         for k in range(3):
-            acc = jnp.where(hits[k], a[0], 0.0)
-            for o in range(1, 6):
-                acc = acc + jnp.where(hits[o + k], a[o], 0.0)
-            wt[k, at, :] = acc.astype(BF16)
+            wt[k, at, :] = jnp.concatenate([top[k], low[k]], axis=0).astype(BF16)
         return carry
 
     lax.fori_loop(0, vocab // BLOCK, spread_in, 0)
@@ -535,12 +558,13 @@
     x1_own[...] = jnp.broadcast_to(jnp.sum(lanes[...].T, axis=0, keepdims=True), (8, rows))
     put_1 = remote(x1_own, x1_in, s_core.at[1], r_core.at[1], (d, s, 1 - t))
     put_1.start()
+    lax.fori_loop(split_at, chans // TILE, pull_back, 0)
     put_1.wait()
     scale = lax.rsqrt((x1_own[...] + x1_in[...]) / D + EPS)
     scale_c = scale.T[:, 0:1]
 
-    def product(at_row):
-        at = pl.ds(pl.multiple_of(at_row, 128), quarter)
+    def product(c):
+        at = pl.ds(c * TILE, TILE)
         normed = (pooled[:, at] * scale_c * gain_ref[:, at]).astype(BF16)
         q[at, :] = mm(normed, g[...], TN).astype(BF16)
 
@@ -549,11 +573,13 @@
     near2 = ((y_near, s, t), (x_near, s, t))
 
     def q_rows(h, first, second):
-        return pl.ds(pl.multiple_of(h * half + first * quarter + second * eighth, eighth), eighth)
-
-    p1 = {}
+        return pl.ds(pl.multiple_of(h * half + first * quarter + second * eighth, BLOCK), eighth)
+
+    p1, done = {}, 0
     for h in range(2):
-        product(h * half + (1 - bit1[h]) * quarter)
+        while done * TILE < (h + 1) * half:
+            product(done)
+            done += 1
         for part in range(2):
             second = bit2[h] if part else 1 - bit2[h]
             p1[h, part] = remote(
@@ -561,38 +587,43 @@
                 s_p1.at[h, part], r_p1.at[h, part], near1[h],
             )
             p1[h, part].start()
-    for h in range(2):
-        product(h * half + bit1[h] * quarter)
-
-    take_w.wait()
+    while done * TILE < chans:
+        product(done)
+        done += 1
+    late = slice(first_z, chans)
+    z_first = []
+    for e, ss in enumerate(seq_peers):
+        at = pl.ds(pl.multiple_of(ss * cols, 128), cols)
+        z_first.append(remote(q.at[late, at], zq.at[e], s_zq.at[e], r_zq.at[e], (d, ss, t)))
+        z_first[-1].start()
+
     lanes[...] = jnp.zeros_like(lanes)
 
-    def pull_back(c, carry):
+    def inner_in(c, carry):
         at = pl.ds(pl.multiple_of(c * TILE, TILE), TILE)
-        part = mm(g[...], wq[at, :], NT)
-        ng[:, at] = part
-        gained = part * gain_ref[:, at]
-        gb[:, at] = gained.astype(BF16)
-        inner = pooled[:, at] * gained
+        inner = pooled[:, at] * (ng[:, at] * gain_ref[:, at])
         lanes[...] += inner[:, 0:128] + inner[:, 128:256]
         return carry
 
-    lax.fori_loop(0, chans // TILE, pull_back, 0)
+    lax.fori_loop(0, chans // TILE, inner_in, 0)
     found = []
     for source in (gb, pb):
+        rr[...] = mm(tk[...], source[...], NT)
+
+        def select(n, accs):
+            at = pl.multiple_of(n * 8, 8)
+            v = lax.broadcasted_iota(jnp.int32, (8, rows), 0) + n * 8
+            accs = list(accs)
+            lines = [rr[pl.ds(k * vocab + at, 8), :] for k in range(3)]
+            for j in range(8):
+                hit = idm_s[j] == v
+                for k in range(3):
+                    if 0 <= j - k < 6:
+                        accs[j - k] = accs[j - k] + jnp.where(hit, lines[k], 0.0)
+            return tuple(accs)
+
         sums = tuple(jnp.zeros((8, rows), F32) for o in range(6))
-        for k in range(3):
-            rr[...] = mm(tk[k * vocab : (k + 1) * vocab, :], source[...], NT)
-
-            def select(n, accs, k=k):
-                line = rr[pl.ds(pl.multiple_of(n * 8, 8), 8), :]
-                v = lax.broadcasted_iota(jnp.int32, (8, rows), 0) + n * 8
-                return tuple(
-                    accs[o] + jnp.where(idm_s[o + k : o + k + 1, :] == v, line, 0.0)
-                    for o in range(6)
-                )
-
-            sums = lax.fori_loop(0, vocab // 8, select, sums)
+        sums = lax.fori_loop(0, vocab // 8, select, sums)
         found += [jnp.sum(acc, axis=0, keepdims=True) for acc in sums]
     found.append(jnp.sum(lanes[...].T, axis=0, keepdims=True))
     found.append(jnp.zeros((3, rows), F32))
@@ -625,18 +656,17 @@
     sgrad = probs * (pgrad - over_blocks(probs * pgrad))
     ds = [jnp.sum(sgrad * w, axis=0, keepdims=True) for w in w8]
 
+    for o in range(6):
+        a_s[o] = jnp.broadcast_to(ds[o], (8, rows))
+
     def count_in(n, carry):
-        at = pl.ds(pl.multiple_of(n * BLOCK, BLOCK), BLOCK)
-        v = lax.broadcasted_iota(jnp.int32, (BLOCK, rows), 0) + n * BLOCK
-        hits = [idm_s[j : j + 1, :] == v for j in range(8)]
+        at = pl.ds(pl.multiple_of(n * 8, 8), 8)
+        accs = spread_rows(n * 8)
         for k in range(3):
-            acc = jnp.where(hits[k], ds[0], 0.0)
-            for o in range(1, 6):
-                acc = acc + jnp.where(hits[o + k], ds[o], 0.0)
-            hist[k, at, :] = jnp.broadcast_to(jnp.sum(acc, axis=1, keepdims=True), (BLOCK, 128))
+            hist[k, at, :] = jnp.broadcast_to(jnp.sum(accs[k], axis=1, keepdims=True), (8, 128))
         return carry
 
-    lax.fori_loop(0, vocab // BLOCK, count_in, 0)
+    lax.fori_loop(0, vocab // 8, count_in, 0)
     pull_c = jnp.broadcast_to(pull, (8, rows)).T[:, 0:1]
 
     def table_step(c, carry):
@@ -662,22 +692,22 @@
 
     lax.fori_loop(0, chans // TILE, table_step, 0)
 
-    t_rs, sm_z = [], []
-    for e, dd in enumerate(dp_peers):
-        block = tb.at[pl.ds(pl.multiple_of(dd * t_dp, t_dp), t_dp)]
-        t_rs.append(remote(block, tr.at[d], s_t.at[e], r_t.at[e], (dd, s, t)))
-        t_rs[-1].start()
+    t_rs, sm_z = {}, []
+    turns = [(s + e + 1) % n_seq for e in range(n_seq)]
+    for e, j in enumerate(turns):
+        for n, dd in enumerate(dp_peers):
+            block = tb.at[pl.ds(pl.multiple_of(dd * t_dp + j * t_seq, t_seq), t_seq)]
+            t_rs[e, n] = remote(block, tr.at[e, n], s_trs.at[e, n], r_trs.at[e, n], (dd, s, t))
+            t_rs[e, n].start()
     for e, ss in enumerate(seq_peers):
         sm_z.append(remote(sm, sz.at[s], s_sm.at[e], r_sm.at[e], (d, ss, t)))
         sm_z[-1].start()
-    tr[d] = tb[pl.ds(pl.multiple_of(d * t_dp, t_dp), t_dp), :]
     sz[s] = sm[...]
 
     for h in range(2):
         p1[h, 1].wait_recv()
     q_z = {}
-    for e in range(n_seq):
-        j = (s + e + 1) % n_seq
+    for e, j in enumerate(turns):
         at = pl.ds(pl.multiple_of(j * cols, 128), cols)
         for h in range(2):
             p2[h, e].wait_recv()
@@ -693,18 +723,30 @@
             else:
                 own_z[h] = block
 
-    for copy in t_rs:
+    for copy in z_first:
         copy.wait_recv()
-    acc = tr[0].astype(F32)
-    for n in range(1, 4):
-        acc = acc + tr[n].astype(F32)
-    ts[...] = acc.astype(BF16)
-    t_z = []
-    for e, ss in enumerate(seq_peers):
-        block = ts.at[pl.ds(pl.multiple_of(ss * t_seq, t_seq), t_seq)]
-        t_z.append(remote(block, tz.at[s], s_t.at[3 + e], r_t.at[3 + e], (d, ss, t)))
-        t_z[-1].start()
-    tz[s] = ts[pl.ds(pl.multiple_of(s * t_seq, t_seq), t_seq), :]
+    block = q[late, pl.ds(pl.multiple_of(s * cols, 128), cols)].astype(F32)
+    for e in range(n_seq - 1):
+        block = block + zq[e].astype(F32)
+    zs[...] = block.astype(BF16)
+    z_rs = []
+    for n, dd in enumerate(dp_peers):
+        rows_n = pl.ds(pl.multiple_of(dd * step_z, BLOCK), step_z)
+        z_rs.append(remote(zs.at[rows_n], zd.at[n], s_zd.at[n], r_zd.at[n], (dd, s, t)))
+        z_rs[-1].start()
+
+    t_z = {}
+    for e, j in enumerate(turns):
+        acc = tb[pl.ds(pl.multiple_of(d * t_dp + j * t_seq, t_seq), t_seq), :].astype(F32)
+        for n in range(3):
+            t_rs[e, n].wait_recv()
+            acc = acc + tr[e, n].astype(F32)
+        if e < n_seq - 1:
+            ts[e] = acc.astype(BF16)
+            t_z[e] = remote(ts.at[e], tz.at[e], s_tz.at[e], r_tz.at[e], (d, j, t))
+            t_z[e].start()
+        else:
+            own_t[...] = acc
 
     for copy in sm_z:
         copy.wait_recv()
@@ -713,11 +755,25 @@
         acc = acc + sz[n]
     sd[d] = acc
     sm_d = []
-    for e, dd in enumerate(dp_peers):
-        sm_d.append(remote(sd.at[d], sd.at[d], s_sm.at[3 + e], r_sm.at[3 + e], (dd, s, t)))
+    for n, dd in enumerate(dp_peers):
+        sm_d.append(remote(sd.at[d], sd.at[d], s_sm.at[3 + n], r_sm.at[3 + n], (dd, s, t)))
         sm_d[-1].start()
 
-    q_ag = []
+    ag = []
+
+    def share(out, mine, send, recv):
+        for n, dd in enumerate(dp_peers):
+            ag.append(remote(out.at[mine], out.at[mine], send.at[n], recv.at[n], (dd, s, t)))
+            ag[-1].start()
+
+    block = zs[pl.ds(pl.multiple_of(d * step_z, BLOCK), step_z), :].astype(F32)
+    for n in range(3):
+        z_rs[n].wait_recv()
+        block = block + zd[n].astype(F32)
+    mine = pl.ds(pl.multiple_of(first_z + d * step_z, BLOCK), step_z)
+    query_ref[mine, :] = block.astype(BF16)
+    share(query_ref, mine, s_ag.at[2], r_ag.at[2])
+
     for h in range(2):
         block = own_z[h]
         for e in range(n_seq - 1):
@@ -725,44 +781,38 @@
             block = block + zr[h, e].astype(F32)
         mine = q_rows(h, bit1[h], bit2[h])
         query_ref[mine, :] = block.astype(BF16)
-        for e, dd in enumerate(dp_peers):
-            q_ag.append(
-                remote(
-                    query_ref.at[mine], query_ref.at[mine], s_ag.at[h, e], r_ag.at[h, e], (dd, s, t)
-                )
-            )
-            q_ag[-1].start()
-
-    for copy in t_z:
-        copy.wait_recv()
-    acc = tz[0].astype(F32)
-    for n in range(1, n_seq):
-        acc = acc + tz[n].astype(F32)
-    mine = pl.ds(pl.multiple_of(d * t_dp + s * t_seq, t_seq), t_seq)
+        share(query_ref, mine, s_ag.at[h], r_ag.at[h])
+
+    acc = own_t[...]
+    for e in range(n_seq - 1):
+        t_z[e].wait_recv()
+        acc = acc + tz[e].astype(F32)
+
+    def table_rows(j):
+        return pl.ds(pl.multiple_of(d * t_dp + j * t_seq, t_seq), t_seq)
+
+    mine = table_rows(s)
     tab_ref[mine, :] = acc.astype(BF16)
     t_back = []
     for e, ss in enumerate(seq_peers):
         t_back.append(
-            remote(tab_ref.at[mine], tab_ref.at[mine], s_t.at[6 + e], r_t.at[6 + e], (d, ss, t))
+            remote(tab_ref.at[mine], tab_ref.at[mine], s_tb.at[e], r_tb.at[e], (d, ss, t))
         )
         t_back[-1].start()
-    for copy in t_back:
-        copy.wait_recv()
-    t_ag = []
-    mine = pl.ds(pl.multiple_of(d * t_dp, t_dp), t_dp)
-    for e, dd in enumerate(dp_peers):
-        t_ag.append(
-            remote(tab_ref.at[mine], tab_ref.at[mine], s_t.at[9 + e], r_t.at[9 + e], (dd, s, t))
-        )
-        t_ag[-1].start()
+    share(tab_ref, mine, s_ta.at[n_seq - 1], r_ta.at[n_seq - 1])
+    for e in range(n_seq - 1):
+        t_back[e].wait_recv()
+        share(tab_ref, table_rows((s + n_seq - 1 - e) % n_seq), s_ta.at[e], r_ta.at[e])
 
     for copy in sm_d:
         copy.wait_recv()
     small_ref[...] = (sd[0] + sd[1]) + (sd[2] + sd[3])
-    for copy in q_ag + t_ag:
+    for copy in ag:
         copy.wait_recv()
-    started = list(p1.values()) + list(p2.values()) + list(q_z.values())
-    for copy in started + t_rs + t_z + t_back + t_ag + sm_z + sm_d + q_ag:
+    for group in (p1, p2, q_z, t_rs, t_z):
+        for copy in group.values():
+            copy.wait_send()
+    for copy in z_first + z_rs + t_back + sm_z + sm_d + ag:
         copy.wait_send()
 
 
@@ -791,7 +841,9 @@
     width = query_grad.shape[2]
     n_seq = lax.axis_size("seq")
     cols = width // n_seq
-    part, t_dp = chans // 8, vocab // 4
+    first_z = 3 * chans // 4
+    part, t_dp = first_z // 8, vocab // 4
+    t_seq, step_z, others = t_dp // n_seq, (chans - first_z) // 4, n_seq - 1
     vm = pl.BlockSpec(memory_space=pltpu.VMEM)
     sm = pl.BlockSpec(memory_space=pltpu.SMEM)
     hbm = pl.BlockSpec(memory_space=pl.ANY)
@@ -809,19 +861,26 @@
             V((chans, width), BF16), V((rows, width), BF16), V((3 * vocab, chans), BF16),
             V((3, vocab, rows), BF16), V((rows, 3 * vocab), BF16), V((rows, chans), F32),
             V((rows, chans), F32), V((rows, chans), BF16), V((rows, chans), BF16),
-            V((chans, width), BF16), V((8, rows), jnp.int32), V((6, 8, rows), F32),
-            V((8, rows), F32), V((3, vocab, 128), F32), V((vocab, rows), F32), V((rows, 128), F32),
+            V((chans, width), BF16), V((8, 8, rows), jnp.int32), V((6, 8, rows), F32),
+            V((6, 8, rows), F32), V((8, rows), F32), V((3, vocab, 128), F32),
+            V((3 * vocab, rows), F32), V((rows, 128), F32),
             V((8, vocab), F32), V((8, vocab), F32), V((2, 1, 128), jnp.int32),
             V((8, rows), F32), V((8, rows), F32), V((16, rows), F32), V((16, rows), F32),
             V((2, 2, part, width), BF16), V((2, part, width), BF16), V((2, part, width), BF16),
-            V((2, n_seq - 1, part, cols), BF16), V((2, n_seq - 1, part, cols), BF16),
-            V((2, part, cols), F32), V((vocab, chans), BF16), V((4, t_dp, chans), BF16),
-            V((t_dp, chans), BF16), V((n_seq, t_dp // n_seq, chans), BF16),
-            V((8, chans), F32), V((n_seq, 8, chans), F32), V((4, 8, chans), F32),
+            V((2, others, part, cols), BF16), V((2, others, part, cols), BF16),
+            V((2, part, cols), F32), V((others, chans - first_z, cols), BF16),
+            V((chans - first_z, cols), BF16), V((3, step_z, cols), BF16),
+            V((vocab, chans), BF16), V((n_seq, 3, t_seq, chans), BF16),
+            V((others, t_seq, chans), BF16), V((others, t_seq, chans), BF16),
+            V((t_seq, chans), F32), V((8, chans), F32), V((n_seq, 8, chans), F32),
+            V((4, 8, chans), F32),
             DMA((2,)), DMA((2,)), DMA((2,)), DMA((3,)), DMA((3,)),
             DMA((2, 2)), DMA((2, 2)), DMA((2, n_seq)), DMA((2, n_seq)),
-            DMA((2, n_seq - 1)), DMA((2, n_seq - 1)), DMA((2, 3)), DMA((2, 3)),
-            DMA((12,)), DMA((12,)), DMA((6,)), DMA((6,)),
+            DMA((2, others)), DMA((2, others)), DMA((3, 3)), DMA((3, 3)),
+            DMA((others,)), DMA((others,)), DMA((3,)), DMA((3,)),
+            DMA((n_seq, 3)), DMA((n_seq, 3)), DMA((others,)), DMA((others,)),
+            DMA((others,)), DMA((others,)), DMA((n_seq, 3)), DMA((n_seq, 3)),
+            DMA((6,)), DMA((6,)),
         ],
         compiler_params=pltpu.CompilerParams(collective_id=0, has_side_effects=True),
         name="fused",

time: 66.2 us -> 59.9 us (0.905)
  Pallas kernels: 64.8 us -> 58.5 us
    pallas_call x1, Pallas kernels: 62.5 us -> 56.2 us  [fused_body(): pl.pallas_call(fused_kernel, out_shape=(jax.ShapeDtypeStruct((vocab, chan...]
where the time goes in v3:
time: 59.9 us; the launch traced here: 59.7 us
  Pallas kernels  58.5 us (98%)
  between operations  1.29 us (2%)
    pallas_call x1, Pallas kernels, fused_body(): pl.pallas_call(fused_kernel, out_shape=(jax.ShapeDtypeStruct((vocab, chan...  56.2 us
    pallas_call x1, Pallas kernels, fused_body(): pl.pallas_call(finish_kernel, out_shape=(jax.ShapeDtypeStruct((vocab, cha...  2.23 us

profile of v3, /device:TPU:0, one launch (start us, length us, event | category | flops | bytes accessed | tf_op | source)
XLA Modules:
  0.0 59.7 jit_solution(2552818819025518667)
XLA Ops:
  1.3 56.2 %fused.1 = (bf16[256,1024]{1,0:T(8,128)(2,1)}, f32[8,1024]{1,0:T(8,128)}, bf16[1024,256]{1,0:T(8,128)(2,1)}) custom-call(s32[1]{0:T(128)S(6)} %copy.13.pad_ref, s32[1,1024]{1,0:T(1,128)} %ids_ref.1, bf16[256,1024]{1,0:T(8,128)(2,1)} %table_ref.1, f32[3,1024]{1,0:T(4,128)} %cw_ref.1, f32[1,1024]{1,0:T(1,128)} %bitcast.6, f32[1,1024]{1,0:T(1,128)} %bitcast.7, ...), custom_call_target="tpu_custom_call" | custom-call | tf_op jit(solution)/shard_map/fused/pallas_call | solution.py:851
  57.5 2.2 %finish.1 = (bf16[256,1024]{1,0:T(8,128)(2,1)}, f32[3,1024]{1,0:T(4,128)}, f32[1,1024]{1,0:T(1,128)}, f32[1,1024]{1,0:T(1,128)}, bf16[1024,256]{1,0:T(8,128)(2,1)}) custom-call(bf16[256,1024]{1,0:T(8,128)(2,1)} %get-tuple-element.13.tab_ref, f32[8,1024]{1,0:T(8,128)} %get-tuple-element.14.small_ref, bf16[1024,256]{1,0:T(8,128)(2,1)} %get-tuple-element.15.query_ref), custom_call_target="tpu_custom_call" | custom-call | tf_op jit(solution)/shard_map/finish/pallas_call | solution.py:891

commit v4 on v3

--- a/solution.py
+++ b/solution.py
@@ -344,11 +344,11 @@
 
 
 def fused_kernel(
-    pad_ref, ids_ref, table_ref, cw_ref, sw_ref, gain_ref, wq_hbm, g_hbm,
+    pad_ref, ids_ref, table_hbm, cw_ref, sw_ref, gain_ref, wq_hbm, g_hbm,
     tab_ref, small_ref, query_ref,
-    wq, g, tk, wt, wcat, pooled, ng, gb, pb, q, idm_s, a_s, w8_s, probs_s, hist, rr, lanes,
+    table_ref, wq, g, tk, wt, wcat, pooled, ng, gb, pb, q, idm_s, a_s, w8_s, probs_s, hist, rr, lanes,
     p_own, p_in, halo, x1_own, x1_in, x2_own, x2_in,
-    r1, s2, r2, zb, zr, own_z, zq, zs, zd, tb, tr, ts, tz, own_t, sm, sz, sd,
+    r1, s2, r2, zb, zr, own_z, late, zq, zs, zd, tb, tr, ts, tz, own_t, sm, sz, sd,
     in_sem, s_halo, r_halo, s_core, r_core, s_p1, r_p1, s_p2, r_p2, s_z, r_z, s_ag, r_ag,
     s_zq, r_zq, s_zd, r_zd, s_trs, r_trs, s_tz, r_tz, s_tb, r_tb, s_ta, r_ta, s_sm, r_sm,
 ):
@@ -381,6 +381,8 @@
 
     take_g = pltpu.make_async_copy(g_hbm, g, in_sem.at[0])
     take_w = pltpu.make_async_copy(wq_hbm, wq, in_sem.at[1])
+    take_t = pltpu.make_async_copy(table_hbm, table_ref, in_sem.at[2])
+    take_t.start()
     take_g.start()
     take_w.start()
 
@@ -390,6 +392,7 @@
         pl.semaphore_signal(barrier, inc=1, device_id=peer, device_id_type=MESH)
 
     cs = cw_ref[...] * sw_ref[...]
+    take_t.wait()
     p_own[...] = sum_parts(mm(stacked(pad8(cs)), table_ref[...], NT))
     pl.semaphore_wait(barrier, len(peers))
 
@@ -539,7 +542,7 @@
             wt[k, at, :] = jnp.concatenate([top[k], low[k]], axis=0).astype(BF16)
         return carry
 
-    lax.fori_loop(0, vocab // BLOCK, spread_in, 0)
+    lax.fori_loop(0, vocab // BLOCK, spread_in, 0, unroll=2)
     for k in range(3):
         wcat[:, k * vocab : (k + 1) * vocab] = wt[k].astype(F32).T.astype(BF16)
 
@@ -586,15 +589,16 @@
                 q.at[q_rows(h, 1 - bit1[h], second)], r1.at[h, part],
                 s_p1.at[h, part], r_p1.at[h, part], near1[h],
             )
-            p1[h, part].start()
-    while done * TILE < chans:
-        product(done)
-        done += 1
-    late = slice(first_z, chans)
+        p1[h, 0].start()
+    for c in range(done, chans // TILE):
+        at = pl.ds(c * TILE, TILE)
+        normed = (pooled[:, at] * scale_c * gain_ref[:, at]).astype(BF16)
+        whole = mm(normed, g[...], TN).astype(BF16)
+        for j in range(n_seq):
+            late[j, (c - done) * TILE : (c - done + 1) * TILE] = whole[:, j * cols : (j + 1) * cols]
     z_first = []
     for e, ss in enumerate(seq_peers):
-        at = pl.ds(pl.multiple_of(ss * cols, 128), cols)
-        z_first.append(remote(q.at[late, at], zq.at[e], s_zq.at[e], r_zq.at[e], (d, ss, t)))
+        z_first.append(remote(late.at[ss], zq.at[e], s_zq.at[e], r_zq.at[e], (d, ss, t)))
         z_first[-1].start()
 
     lanes[...] = jnp.zeros_like(lanes)
@@ -623,23 +627,26 @@
             return tuple(accs)
 
         sums = tuple(jnp.zeros((8, rows), F32) for o in range(6))
-        sums = lax.fori_loop(0, vocab // 8, select, sums)
+        sums = lax.fori_loop(0, vocab // 8, select, sums, unroll=2)
         found += [jnp.sum(acc, axis=0, keepdims=True) for acc in sums]
     found.append(jnp.sum(lanes[...].T, axis=0, keepdims=True))
     found.append(jnp.zeros((3, rows), F32))
     x2_own[...] = jnp.concatenate(found, axis=0)
     put_2 = remote(x2_own, x2_in, s_core.at[2], r_core.at[2], (d, s, 1 - t))
     put_2.start()
+    for h in range(2):
+        p1[h, 0].wait_send()
+        p1[h, 1].start()
 
     p2 = {}
     for h in range(2):
         p1[h, 0].wait_recv()
         rows_h = q_rows(h, bit1[h], 1 - bit2[h])
-        s2[h] = (q[rows_h, :].astype(F32) + r1[h, 0].astype(F32)).astype(BF16)
         for e in range(n_seq):
             at = pl.ds(pl.multiple_of((s + e + 1) % n_seq * cols, 128), cols)
+            s2[h, e] = (q[rows_h, at].astype(F32) + r1[h, 0, :, at].astype(F32)).astype(BF16)
             p2[h, e] = remote(
-                s2.at[h, :, at], r2.at[h, :, at], s_p2.at[h, e], r_p2.at[h, e], near2[h]
+                s2.at[h, e], r2.at[h, e], s_p2.at[h, e], r_p2.at[h, e], near2[h]
             )
             p2[h, e].start()
 
@@ -663,10 +670,15 @@
         at = pl.ds(pl.multiple_of(n * 8, 8), 8)
         accs = spread_rows(n * 8)
         for k in range(3):
-            hist[k, at, :] = jnp.broadcast_to(jnp.sum(accs[k], axis=1, keepdims=True), (8, 128))
+            fold = accs[k][:, 0:128]
+            for n in range(1, rows // 128):
+                fold = fold + accs[k][:, n * 128 : (n + 1) * 128]
+            hist[k, at, :] = fold
         return carry
 
-    lax.fori_loop(0, vocab // 8, count_in, 0)
+    lax.fori_loop(0, vocab // 8, count_in, 0, unroll=2)
+    for k in range(3):
+        hist[k] = jnp.broadcast_to(jnp.sum(hist[k], axis=1, keepdims=True), (vocab, 128))
     pull_c = jnp.broadcast_to(pull, (8, rows)).T[:, 0:1]
 
     def table_step(c, carry):
@@ -694,15 +706,23 @@
 
     t_rs, sm_z = {}, []
     turns = [(s + e + 1) % n_seq for e in range(n_seq)]
-    for e, j in enumerate(turns):
+    chunk = chans // n_seq
+
+    def part_of(j):
+        return pl.ds(pl.multiple_of(j * chunk, 128), chunk)
+
+    def send_table(e):
         for n, dd in enumerate(dp_peers):
-            block = tb.at[pl.ds(pl.multiple_of(dd * t_dp + j * t_seq, t_seq), t_seq)]
+            block = tb.at[pl.ds(pl.multiple_of(dd * t_dp + turns[e] * t_seq, t_seq), t_seq)]
             t_rs[e, n] = remote(block, tr.at[e, n], s_trs.at[e, n], r_trs.at[e, n], (dd, s, t))
             t_rs[e, n].start()
+
+    send_table(0)
     for e, ss in enumerate(seq_peers):
-        sm_z.append(remote(sm, sz.at[s], s_sm.at[e], r_sm.at[e], (d, ss, t)))
+        sm_z.append(
+            remote(sm.at[:, part_of(ss)], sz.at[e], s_sm.at[e], r_sm.at[e], (d, ss, t))
+        )
         sm_z[-1].start()
-    sz[s] = sm[...]
 
     for h in range(2):
         p1[h, 1].wait_recv()
@@ -713,7 +733,7 @@
             p2[h, e].wait_recv()
             rows_h = q_rows(h, bit1[h], bit2[h])
             block = q[rows_h, at].astype(F32) + r1[h, 1, :, at].astype(F32)
-            block = block + r2[h, :, at].astype(F32)
+            block = block + r2[h, e].astype(F32)
             if e < n_seq - 1:
                 zb[h, e] = block.astype(BF16)
                 q_z[h, e] = remote(
@@ -722,10 +742,14 @@
                 q_z[h, e].start()
             else:
                 own_z[h] = block
+        if e % 2:
+            send_table(e // 2 + 1)
+    for e in range(n_seq // 2 + 1, n_seq):
+        send_table(e)
 
     for copy in z_first:
         copy.wait_recv()
-    block = q[late, pl.ds(pl.multiple_of(s * cols, 128), cols)].astype(F32)
+    block = late[s].astype(F32)
     for e in range(n_seq - 1):
         block = block + zq[e].astype(F32)
     zs[...] = block.astype(BF16)
@@ -748,11 +772,10 @@
         else:
             own_t[...] = acc
 
-    for copy in sm_z:
+    acc = sm[:, part_of(s)]
+    for e, copy in enumerate(sm_z):
         copy.wait_recv()
-    acc = sz[0]
-    for n in range(1, n_seq):
-        acc = acc + sz[n]
+        acc = acc + sz[e]
     sd[d] = acc
     sm_d = []
     for n, dd in enumerate(dp_peers):
@@ -761,27 +784,53 @@
 
     ag = []
 
-    def share(out, mine, send, recv):
-        for n, dd in enumerate(dp_peers):
-            ag.append(remote(out.at[mine], out.at[mine], send.at[n], recv.at[n], (dd, s, t)))
+    def share(out, rows_of, send, recv, via=None):
+        targets = dp_peers if via is None else dp_peers[:2]
+        copies = []
+        for n, dd in enumerate(targets):
+            mine = out.at[rows_of(d)]
+            copies.append(remote(mine, mine, send.at[n], recv.at[n], (dd, s, t)))
+            copies[-1].start()
+        ag.extend(copy for n, copy in enumerate(copies) if n != via)
+        if via is None:
+            return None
+
+        def relay():
+            copies[via].wait_recv()
+            passed.append(copies[via])
+            theirs = out.at[rows_of(dp_peers[via])]
+            ag.append(
+                remote(theirs, theirs, send.at[2], recv.at[2], (dp_peers[1 - via], s, t))
+            )
             ag[-1].start()
+
+        return relay
+
+    passed = []
 
     block = zs[pl.ds(pl.multiple_of(d * step_z, BLOCK), step_z), :].astype(F32)
     for n in range(3):
         z_rs[n].wait_recv()
         block = block + zd[n].astype(F32)
-    mine = pl.ds(pl.multiple_of(first_z + d * step_z, BLOCK), step_z)
-    query_ref[mine, :] = block.astype(BF16)
-    share(query_ref, mine, s_ag.at[2], r_ag.at[2])
-
+    def late_rows(dd):
+        return pl.ds(pl.multiple_of(first_z + dd * step_z, BLOCK), step_z)
+
+    query_ref[late_rows(d), :] = block.astype(BF16)
+    share(query_ref, late_rows, s_ag.at[2], r_ag.at[2])
+
+    relays = []
     for h in range(2):
         block = own_z[h]
         for e in range(n_seq - 1):
             q_z[h, e].wait_recv()
             block = block + zr[h, e].astype(F32)
-        mine = q_rows(h, bit1[h], bit2[h])
-        query_ref[mine, :] = block.astype(BF16)
-        share(query_ref, mine, s_ag.at[h], r_ag.at[h])
+
+        def early_rows(dd, h=h):
+            bits = (dd % 2, dd // 2)
+            return q_rows(h, bits[h], bits[1 - h])
+
+        query_ref[early_rows(d), :] = block.astype(BF16)
+        relays.append(share(query_ref, early_rows, s_ag.at[h], r_ag.at[h], h))
 
     acc = own_t[...]
     for e in range(n_seq - 1):
@@ -789,9 +838,9 @@
         acc = acc + tz[e].astype(F32)
 
     def table_rows(j):
-        return pl.ds(pl.multiple_of(d * t_dp + j * t_seq, t_seq), t_seq)
-
-    mine = table_rows(s)
+        return lambda dd: pl.ds(pl.multiple_of(dd * t_dp + j * t_seq, t_seq), t_seq)
+
+    mine = table_rows(s)(d)
     tab_ref[mine, :] = acc.astype(BF16)
     t_back = []
     for e, ss in enumerate(seq_peers):
@@ -799,20 +848,29 @@
             remote(tab_ref.at[mine], tab_ref.at[mine], s_tb.at[e], r_tb.at[e], (d, ss, t))
         )
         t_back[-1].start()
-    share(tab_ref, mine, s_ta.at[n_seq - 1], r_ta.at[n_seq - 1])
+    late_relay = share(tab_ref, table_rows(s), s_ta.at[n_seq - 1], r_ta.at[n_seq - 1], 0)
+    for copy in sm_d:
+        copy.wait_recv()
+    small_ref[:, part_of(s)] = (sd[0] + sd[1]) + (sd[2] + sd[3])
+    for e, ss in enumerate(seq_peers):
+        block = small_ref.at[:, part_of(s)]
+        sm_d.append(remote(block, block, s_sm.at[6 + e], r_sm.at[6 + e], (d, ss, t)))
+        sm_d[-1].start()
     for e in range(n_seq - 1):
         t_back[e].wait_recv()
         share(tab_ref, table_rows((s + n_seq - 1 - e) % n_seq), s_ta.at[e], r_ta.at[e])
-
-    for copy in sm_d:
+        if e < 2:
+            relays.pop(0)()
+    late_relay()
+
+    for copy in sm_d[3:] + ag:
         copy.wait_recv()
-    small_ref[...] = (sd[0] + sd[1]) + (sd[2] + sd[3])
-    for copy in ag:
-        copy.wait_recv()
-    for group in (p1, p2, q_z, t_rs, t_z):
+    for h in range(2):
+        p1[h, 1].wait_send()
+    for group in (p2, q_z, t_rs, t_z):
         for copy in group.values():
             copy.wait_send()
-    for copy in z_first + z_rs + t_back + sm_z + sm_d + ag:
+    for copy in z_first + z_rs + t_back + sm_z + sm_d + ag + passed:
         copy.wait_send()
 
 
@@ -850,37 +908,34 @@
     V, DMA = pltpu.VMEM, pltpu.SemaphoreType.DMA
     tab, small, query = pl.pallas_call(
         fused_kernel,
-        out_shape=(
-            jax.ShapeDtypeStruct((vocab, chans), BF16),
-            jax.ShapeDtypeStruct((8, chans), F32),
-            jax.ShapeDtypeStruct((chans, cols), BF16),
-        ),
-        in_specs=[sm] + [vm] * 5 + [hbm] * 2,
+        out_shape=(V((vocab, chans), BF16), V((8, chans), F32), V((chans, cols), BF16)),
+        in_specs=[sm, vm, hbm] + [vm] * 3 + [hbm] * 2,
         out_specs=(vm,) * 3,
         scratch_shapes=[
+            V((vocab, chans), BF16),
             V((chans, width), BF16), V((rows, width), BF16), V((3 * vocab, chans), BF16),
             V((3, vocab, rows), BF16), V((rows, 3 * vocab), BF16), V((rows, chans), F32),
             V((rows, chans), F32), V((rows, chans), BF16), V((rows, chans), BF16),
-            V((chans, width), BF16), V((8, 8, rows), jnp.int32), V((6, 8, rows), F32),
+            V((first_z, width), BF16), V((8, 8, rows), jnp.int32), V((6, 8, rows), F32),
             V((6, 8, rows), F32), V((8, rows), F32), V((3, vocab, 128), F32),
             V((3 * vocab, rows), F32), V((rows, 128), F32),
             V((8, vocab), F32), V((8, vocab), F32), V((2, 1, 128), jnp.int32),
             V((8, rows), F32), V((8, rows), F32), V((16, rows), F32), V((16, rows), F32),
-            V((2, 2, part, width), BF16), V((2, part, width), BF16), V((2, part, width), BF16),
+            V((2, 2, part, width), BF16), V((2, n_seq, part, cols), BF16), V((2, n_seq, part, cols), BF16),
             V((2, others, part, cols), BF16), V((2, others, part, cols), BF16),
-            V((2, part, cols), F32), V((others, chans - first_z, cols), BF16),
+            V((2, part, cols), F32), V((n_seq, chans - first_z, cols), BF16), V((others, chans - first_z, cols), BF16),
             V((chans - first_z, cols), BF16), V((3, step_z, cols), BF16),
             V((vocab, chans), BF16), V((n_seq, 3, t_seq, chans), BF16),
             V((others, t_seq, chans), BF16), V((others, t_seq, chans), BF16),
-            V((t_seq, chans), F32), V((8, chans), F32), V((n_seq, 8, chans), F32),
-            V((4, 8, chans), F32),
-            DMA((2,)), DMA((2,)), DMA((2,)), DMA((3,)), DMA((3,)),
+            V((t_seq, chans), F32), V((8, chans), F32), V((others, 8, chans // n_seq), F32),
+            V((4, 8, chans // n_seq), F32),
+            DMA((3,)), DMA((2,)), DMA((2,)), DMA((3,)), DMA((3,)),
             DMA((2, 2)), DMA((2, 2)), DMA((2, n_seq)), DMA((2, n_seq)),
             DMA((2, others)), DMA((2, others)), DMA((3, 3)), DMA((3, 3)),
             DMA((others,)), DMA((others,)), DMA((3,)), DMA((3,)),
             DMA((n_seq, 3)), DMA((n_seq, 3)), DMA((others,)), DMA((others,)),
             DMA((others,)), DMA((others,)), DMA((n_seq, 3)), DMA((n_seq, 3)),
-            DMA((6,)), DMA((6,)),
+            DMA((9,)), DMA((9,)),
         ],
         compiler_params=pltpu.CompilerParams(collective_id=0, has_side_effects=True),
         name="fused",
@@ -900,7 +955,7 @@
         in_specs=[vm] * 3,
         out_specs=(vm,) * 5,
         name="finish",
-    )(tab, small, query)
+    )(*(pltpu.with_memory_space_constraint(part, pltpu.VMEM) for part in (tab, small, query)))
 
 
 def fused_outer(*args):

time: 59.9 us -> 56.2 us (0.938)
  Pallas kernels: 58.5 us -> 54.6 us
    pallas_call x1, Pallas kernels: 56.2 us -> 53.6 us  [fused_body(): pl.pallas_call(fused_kernel, out_shape=(V((vocab, chans), BF16), V((8, ch...]
    pallas_call x1, Pallas kernels: 2.23 us -> 1.04 us  [fused_body(): pl.pallas_call(finish_kernel, out_shape=(jax.ShapeDtypeStruct((vocab, cha...]
where the time goes in v4:
time: 56.2 us; the launch traced here: 55.9 us
  Pallas kernels  54.6 us (97%)
  between operations  1.29 us (2%)
    pallas_call x1, Pallas kernels, fused_body(): pl.pallas_call(fused_kernel, out_shape=(V((vocab, chans), BF16), V((8, ch...  53.6 us

profile of v4, /device:TPU:0, one launch (start us, length us, event | category | flops | bytes accessed | tf_op | source)
XLA Modules:
  0.0 55.9 jit_solution(7221969446189866440)
XLA Ops:
  1.3 53.6 %fused.1 = (bf16[256,1024]{1,0:T(8,128)(2,1)S(1)}, f32[8,1024]{1,0:T(8,128)S(1)}, bf16[1024,256]{1,0:T(8,128)(2,1)S(1)}) custom-call(s32[1]{0:T(128)S(6)} %copy.13.pad_ref, s32[1,1024]{1,0:T(1,128)} %ids_ref.1, bf16[256,1024]{1,0:T(8,128)(2,1)} %table_hbm.1, f32[3,1024]{1,0:T(4,128)} %cw_ref.1, f32[1,1024]{1,0:T(1,128)} %bitcast.6, f32[1,1024]{1,0:T(1,128)} %bitcast.7, ...), custom_call_target="tpu_custom_call" | custom-call | tf_op jit(solution)/shard_map/fused/pallas_call | solution.py:909
  54.8 1.0 %finish.1 = (bf16[256,1024]{1,0:T(8,128)(2,1)}, f32[3,1024]{1,0:T(4,128)}, f32[1,1024]{1,0:T(1,128)}, f32[1,1024]{1,0:T(1,128)}, bf16[1024,256]{1,0:T(8,128)(2,1)}) custom-call(bf16[256,1024]{1,0:T(8,128)(2,1)S(1)} %get-tuple-element.13.tab_ref, f32[8,1024]{1,0:T(8,128)S(1)} %get-tuple-element.14.small_ref, bf16[1024,256]{1,0:T(8,128)(2,1)S(1)} %get-tuple-element.15.query_ref), custom_call_target="tpu_custom_call" | custom-call | tf_op jit(solution)/shard_map/finish/pallas_call | solution.py:946

commit v5 on v4

--- a/solution.py
+++ b/solution.py
@@ -350,7 +350,7 @@
     p_own, p_in, halo, x1_own, x1_in, x2_own, x2_in,
     r1, s2, r2, zb, zr, own_z, late, zq, zs, zd, tb, tr, ts, tz, own_t, sm, sz, sd,
     in_sem, s_halo, r_halo, s_core, r_core, s_p1, r_p1, s_p2, r_p2, s_z, r_z, s_ag, r_ag,
-    s_zq, r_zq, s_zd, r_zd, s_trs, r_trs, s_tz, r_tz, s_tb, r_tb, s_ta, r_ta, s_sm, r_sm,
+    s_zq, r_zq, s_zd, r_zd, s_trs, r_trs, s_tz, r_tz, s_tb, r_tb, s_ta, r_ta, s_ca, r_ca, s_sm, r_sm,
 ):
     d, s, t = lax.axis_index("dp"), lax.axis_index("seq"), lax.axis_index("tensor")
     n_seq = lax.axis_size("seq")
@@ -717,6 +717,9 @@
             t_rs[e, n] = remote(block, tr.at[e, n], s_trs.at[e, n], r_trs.at[e, n], (dd, s, t))
             t_rs[e, n].start()
 
+    def corner_rows(j):
+        return pl.ds(pl.multiple_of(corner * t_dp + j * t_seq, t_seq), t_seq)
+
     send_table(0)
     for e, ss in enumerate(seq_peers):
         sm_z.append(
@@ -784,8 +787,8 @@
 
     ag = []
 
-    def share(out, rows_of, send, recv, via=None):
-        targets = dp_peers if via is None else dp_peers[:2]
+    def share(out, rows_of, send, recv, via=None, near=False):
+        targets = dp_peers if via is None and not near else dp_peers[:2]
         copies = []
         for n, dd in enumerate(targets):
             mine = out.at[rows_of(d)]
@@ -848,7 +851,9 @@
             remote(tab_ref.at[mine], tab_ref.at[mine], s_tb.at[e], r_tb.at[e], (d, ss, t))
         )
         t_back[-1].start()
-    late_relay = share(tab_ref, table_rows(s), s_ta.at[n_seq - 1], r_ta.at[n_seq - 1], 0)
+    share(tab_ref, table_rows(s), s_ta.at[n_seq - 1], r_ta.at[n_seq - 1])
+    crossed = ag.pop()
+    passed.append(crossed)
     for copy in sm_d:
         copy.wait_recv()
     small_ref[:, part_of(s)] = (sd[0] + sd[1]) + (sd[2] + sd[3])
@@ -856,21 +861,28 @@
         block = small_ref.at[:, part_of(s)]
         sm_d.append(remote(block, block, s_sm.at[6 + e], r_sm.at[6 + e], (d, ss, t)))
         sm_d[-1].start()
+    crossed.wait_recv()
+    t_back_c = []
+    for e, ss in enumerate(seq_peers):
+        block = tab_ref.at[corner_rows(s)]
+        t_back_c.append(remote(block, block, s_ca.at[e], r_ca.at[e], (d, ss, t)))
+        t_back_c[-1].start()
     for e in range(n_seq - 1):
         t_back[e].wait_recv()
-        share(tab_ref, table_rows((s + n_seq - 1 - e) % n_seq), s_ta.at[e], r_ta.at[e])
+        share(
+            tab_ref, table_rows((s + n_seq - 1 - e) % n_seq), s_ta.at[e], r_ta.at[e], near=True
+        )
         if e < 2:
             relays.pop(0)()
-    late_relay()
-
-    for copy in sm_d[3:] + ag:
+
+    for copy in sm_d[3:] + ag + t_back_c:
         copy.wait_recv()
     for h in range(2):
         p1[h, 1].wait_send()
     for group in (p2, q_z, t_rs, t_z):
         for copy in group.values():
             copy.wait_send()
-    for copy in z_first + z_rs + t_back + sm_z + sm_d + ag + passed:
+    for copy in z_first + z_rs + t_back + t_back_c + sm_z + sm_d + ag + passed:
         copy.wait_send()
 
 
@@ -935,6 +947,7 @@
             DMA((others,)), DMA((others,)), DMA((3,)), DMA((3,)),
             DMA((n_seq, 3)), DMA((n_seq, 3)), DMA((others,)), DMA((others,)),
             DMA((others,)), DMA((others,)), DMA((n_seq, 3)), DMA((n_seq, 3)),
+            DMA((others,)), DMA((others,)),
             DMA((9,)), DMA((9,)),
         ],
         compiler_params=pltpu.CompilerParams(collective_id=0, has_side_effects=True),

time: 56.2 us -> 54 us (0.961)
  Pallas kernels: 54.6 us -> 52.4 us
    pallas_call x1, Pallas kernels: 53.6 us -> 51.4 us  [fused_body(): pl.pallas_call(fused_kernel, out_shape=(V((vocab, chans), BF16), V((8, ch...]
where the time goes in v5:
time: 54 us; the launch traced here: 53.7 us
  Pallas kernels  52.4 us (97%)
  between operations  1.29 us (2%)
    pallas_call x1, Pallas kernels, fused_body(): pl.pallas_call(fused_kernel, out_shape=(V((vocab, chans), BF16), V((8, ch...  51.4 us

profile of v5, /device:TPU:0, one launch (start us, length us, event | category | flops | bytes accessed | tf_op | source)
XLA Modules:
  0.0 53.7 jit_solution(310555522787302026)
XLA Ops:
  1.3 51.4 %fused.1 = (bf16[256,1024]{1,0:T(8,128)(2,1)S(1)}, f32[8,1024]{1,0:T(8,128)S(1)}, bf16[1024,256]{1,0:T(8,128)(2,1)S(1)}) custom-call(s32[1]{0:T(128)S(6)} %copy.13.pad_ref, s32[1,1024]{1,0:T(1,128)} %ids_ref.1, bf16[256,1024]{1,0:T(8,128)(2,1)} %table_hbm.1, f32[3,1024]{1,0:T(4,128)} %cw_ref.1, f32[1,1024]{1,0:T(1,128)} %bitcast.6, f32[1,1024]{1,0:T(1,128)} %bitcast.7, ...), custom_call_target="tpu_custom_call" | custom-call | tf_op jit(solution)/shard_map/fused/pallas_call | solution.py:921
  52.7 1.0 %finish.1 = (bf16[256,1024]{1,0:T(8,128)(2,1)}, f32[3,1024]{1,0:T(4,128)}, f32[1,1024]{1,0:T(1,128)}, f32[1,1024]{1,0:T(1,128)}, bf16[1024,256]{1,0:T(8,128)(2,1)}) custom-call(bf16[256,1024]{1,0:T(8,128)(2,1)S(1)} %get-tuple-element.13.tab_ref, f32[8,1024]{1,0:T(8,128)S(1)} %get-tuple-element.14.small_ref, bf16[1024,256]{1,0:T(8,128)(2,1)S(1)} %get-tuple-element.15.query_ref), custom_call_target="tpu_custom_call" | custom-call | tf_op jit(solution)/shard_map/finish/pallas_call | solution.py:959
